TPU v7x, 512 devices: a whole 4x8x8 slice. The times are simulated.
512 devices in a mesh: seg: 8 (over x, core), state: 64 (over z, y).
Axes of the slice: x: 4, y: 8, z: 8, core: 2. Of those that a mesh axis runs over, the one named last changes fastest.
Arguments:
- forward_in: float32 [8, 8388608], P('seg', 'state'), may hold values from 0.3 to 28, as said below
- backward_in: float32 [8, 8388608], P('seg', 'state'), may hold values from 0.3 to 28, as said below
- compat_masks: int32 [16, 23], P('seg'), may hold values from 1 to 3
- theta_index: int32 [16, 23], P('seg'), may hold values from 0 to 5
Outputs:
- forward_out: float32 [8, 8388608], P('seg', 'state')
- backward_out: float32 [8, 8388608], P('seg', 'state')
- posterior: float32 [8, 8388608], P('seg', 'state')
- log_scales: float32 [2, 8], P(None, 'seg')
Inputs may be any that keep to these rules, and one draw needn't show every extreme that they name: `compat_masks`: 1 allows anchor 0 only, 2 anchor 1 only, 3 both. `forward_in`: positive. `backward_in`: positive.
All inputs are finite; a program needn't handle non-finite values.
Results may differ from a plain program's by a relative error of at most 0.00011.
Values sent between devices are 32-bit elements; how exact they have to be, the bound alone decides.
No kernel may reach another device: no remote copies, remote signals or barrier semaphores. Data moves between devices by JAX's collectives and lax.ppermute only.
A program may use at most 64 MiB of HBM per device.

v0:
```python
import jax
import jax.numpy as jnp
from jax import lax
from jax.sharding import PartitionSpec as P

PENALTY = 0.5
ERROR_RATE = 0.02
BASE_THETA = 0.01


def side_by_side(arrays, axis, split_dim, concat_dim, along):
    both = jnp.concatenate(arrays, axis=along)
    whole, at, done = (
        lax.all_to_all(both, axis, split_axis=split_dim, concat_axis=concat_dim, tiled=True),
        0,
        [],
    )
    for a in arrays:
        done.append(lax.slice_in_dim(whole, at, at + a.shape[along], axis=along))
        at += a.shape[along]
    return tuple(done)


def copy_for_each(shard, axis):
    copies = jnp.broadcast_to(shard, (lax.axis_size(axis), *shard.shape))
    return lax.all_to_all(copies, axis, split_axis=0, concat_axis=0, tiled=True)


def taken_together(shard, axis):
    everything = copy_for_each(shard, axis)
    return jnp.sum(everything, axis=0)


def in_one(arrays, axis):
    flat, at, done = (jnp.concatenate([a.reshape(-1) for a in arrays]), 0, [])
    so_far = taken_together(flat, axis)
    for a in arrays:
        done.append(so_far[at : at + a.size].reshape(a.shape))
        at += a.size
    return tuple(done)


def passed_along(value, axis, steps):
    count = lax.axis_size(axis)
    first, last = (max(0, -steps), min(count, count - steps))
    return lax.ppermute(value, axis, [(source, source + steps) for source in range(first, last)])


def kron_matrix(thetas):
    count = thetas.shape[0]
    width = 2**count
    row_ids = lax.broadcasted_iota(jnp.int32, (width, width), 0)
    col_ids = lax.broadcasted_iota(jnp.int32, (width, width), 1)
    result = jnp.ones((width, width), jnp.float32)
    for which in range(count):
        agrees = row_ids // 2**which % 2 == col_ids // 2**which % 2
        result = result * jnp.where(agrees, 1.0 - thetas[which], thetas[which])
    return result


def mix_local(vector, thetas_local):
    count = thetas_local.shape[0]
    first_bits = min(7, count)
    current = vector.reshape(-1, 2**first_bits)
    current = jnp.dot(
        current,
        kron_matrix(thetas_local[:first_bits]),
        precision=lax.Precision.HIGHEST,
        preferred_element_type=jnp.float32,
    )
    offset = first_bits
    while offset < count:
        width_bits = min(5, count - offset)
        shaped = current.reshape(-1, 2**width_bits, 2**offset)
        current = jnp.einsum(
            "ij,ojk->oik",
            kron_matrix(thetas_local[offset : offset + width_bits]),
            shaped,
            precision=lax.Precision.HIGHEST,
        )
        offset += width_bits
    return current.reshape(-1)


def mix_rows(matrix, thetas_part):
    return jnp.dot(
        kron_matrix(thetas_part),
        matrix,
        precision=lax.Precision.HIGHEST,
        preferred_element_type=jnp.float32,
    )


def anchor_factors(mask_row):
    anchor_zero = jnp.where(mask_row % 2 == 1, 1.0, PENALTY).astype(jnp.float32)
    anchor_one = jnp.where(mask_row // 2 == 1, 1.0, PENALTY).astype(jnp.float32)
    return (anchor_zero, anchor_one)


def bit_product(anchor_zero, anchor_one, first, last):
    product = jnp.ones((1,), jnp.float32)
    for which in range(first, last):
        pair = jnp.stack([anchor_zero[which], anchor_one[which]])
        product = (pair[:, None] * product[None, :]).reshape(-1)
    return product


def emission(mask_row, local_bits, device_index):
    count = mask_row.shape[0]
    anchor_zero, anchor_one = anchor_factors(mask_row)
    product = bit_product(anchor_zero, anchor_one, 0, local_bits)
    high_factor = jnp.ones((), jnp.float32)
    for which in range(count - local_bits):
        anchor = device_index // 2**which % 2
        high_factor = high_factor * jnp.where(
            anchor == 1, anchor_one[local_bits + which], anchor_zero[local_bits + which]
        )
    return ERROR_RATE + (1.0 - ERROR_RATE) * (high_factor * product)


def emission_columns(mask_row, local_bits, high_count, device_index):
    count = mask_row.shape[0]
    anchor_zero, anchor_one = anchor_factors(mask_row)
    low_bits = local_bits - high_count
    low_part = bit_product(anchor_zero, anchor_one, 0, low_bits)
    own_factor = jnp.ones((), jnp.float32)
    for which in range(high_count):
        anchor = device_index // 2**which % 2
        own_factor = own_factor * jnp.where(
            anchor == 1, anchor_one[low_bits + which], anchor_zero[low_bits + which]
        )
    high_part = bit_product(anchor_zero, anchor_one, local_bits, count)
    table = high_part[:, None] * own_factor * low_part[None, :]
    return ERROR_RATE + (1.0 - ERROR_RATE) * table.reshape(-1)


def shards(forward_in, backward_in, compat_masks, theta_index):
    groups = lax.axis_size("state")
    high_count = groups.bit_length() - 1
    device_index = lax.axis_index("state")
    initial = forward_in[0]
    forward = initial
    backward = backward_in[0]
    local_size = initial.shape[0]
    local_bits = local_size.bit_length() - 1
    low_bits = local_bits - high_count
    total_states = local_size * groups
    thetas = BASE_THETA * 2.0 ** theta_index.astype(jnp.float32)
    markers = compat_masks.shape[0]
    emissions = [
        emission(compat_masks[marker], local_bits, device_index) for marker in range(markers)
    ]
    col_emissions = [
        emission_columns(compat_masks[marker], local_bits, high_count, device_index)
        for marker in range(markers)
    ]
    for marker in range(markers):
        behind = markers - 1 - marker
        if marker % 2 == 0:
            fwd_part = mix_local(forward, thetas[marker][:local_bits]).reshape(groups, -1)
            bwd_part = mix_local(emissions[behind] * backward, thetas[behind][:local_bits]).reshape(
                groups, -1
            )
            fwd_part, bwd_part = side_by_side((fwd_part, bwd_part), "state", 0, 0, 1)
            fwd_part = mix_rows(fwd_part, thetas[marker][local_bits:])
            bwd_part = mix_rows(bwd_part, thetas[behind][local_bits:])
            forward = col_emissions[marker] * fwd_part.reshape(-1)
            backward = bwd_part.reshape(-1)
        else:
            fwd_part = mix_local(forward, thetas[marker][:low_bits]).reshape(groups, -1)
            bwd_part = mix_local(
                col_emissions[behind] * backward, thetas[behind][:low_bits]
            ).reshape(groups, -1)
            fwd_part = mix_rows(fwd_part, thetas[marker][local_bits:])
            bwd_part = mix_rows(bwd_part, thetas[behind][local_bits:])
            fwd_part, bwd_part = (
                lax.all_to_all(fwd_part, "state", split_axis=0, concat_axis=0, tiled=True),
                lax.all_to_all(bwd_part, "state", split_axis=0, concat_axis=0, tiled=True),
            )
            fwd_part = mix_rows(fwd_part, thetas[marker][low_bits:local_bits])
            bwd_part = mix_rows(bwd_part, thetas[behind][low_bits:local_bits])
            forward = emissions[marker] * fwd_part.reshape(-1)
            backward = bwd_part.reshape(-1)
    totals = in_one((jnp.sum(forward), jnp.sum(backward)), "state")
    mean_fwd = totals[0] / total_states
    mean_bwd = totals[1] / total_states
    forward = forward / mean_fwd
    backward = backward / mean_bwd
    log_fwd = jnp.log(mean_fwd)
    log_bwd = jnp.log(mean_bwd)
    received = passed_along(forward, "seg", 1)
    left_side = jnp.where(lax.axis_index("seg") == 0, initial, received)
    product = left_side * backward
    post_total = taken_together(jnp.sum(product), "state")
    posterior = product / (post_total / total_states)
    log_scales = jnp.stack([log_fwd, log_bwd]).reshape(2, 1)
    return (forward[None, :], backward[None, :], posterior[None, :], log_scales)


def solution(mesh):
    placed = (P("seg", "state"), P("seg", "state"), P("seg", None), P("seg", None))
    return jax.shard_map(
        shards,
        mesh=mesh,
        in_specs=placed,
        out_specs=(P("seg", "state"), P("seg", "state"), P("seg", "state"), P(None, "seg")),
        check_vma=False,
    )
```

profile of v0, /device:TPU:6, one launch (start us, length us, event | category | flops | bytes accessed | tf_op | source)
XLA Modules:
  0.0 288.7 jit_solution(5812751685984625805)
XLA Ops:
  8.5 2.7 pad_maximum_fusion.15
  11.5 2.6 pad_maximum_fusion.13
  25.4 2.6 pad_maximum_fusion.3
  28.3 2.7 pad_maximum_fusion.1
  49.6 5.3 %fusion.52 = f32[32,32,128]{2,1,0:T(8,128)S(1)} fusion(f32[32,32,128]{2,1,0:T(8,128)S(1)} %fusion.24, f32[]{:T(128)} %bitcast.83, f32[]{:T(128)S(6)} %sub.805, f32[]{:T(128)} %bitcast.82, f32[]{:T(128)S(6)} %sub.804, f32[]{:T(128)} %bitcast.81, f32[]{:T(128)S(6)} %sub.803, f32[]{:T(128)} %bitcast.80, f32[]{:T(128)S(6)} %sub.802, f32[]{:T(128)} %bitcast.79, ...), kind=kOutput, calls=%fused_computation.140 | convolution fusion | flops 204210176 | bytes 1055544 | tf_op jit(solution)/shard_map/dot_general | solution.py:65
  54.9 3.8 %fusion.117 = f32[32,128,32]{1,2,0:T(8,128)S(1)} fusion(f32[32,32,128]{2,1,0:T(8,128)S(1)} %fusion.52, f32[]{:T(128)} %bitcast.14, f32[]{:T(128)S(6)} %sub.748, f32[]{:T(128)} %bitcast.88, f32[]{:T(128)S(6)} %sub.809, f32[]{:T(128)} %bitcast.87, f32[]{:T(128)S(6)} %sub.808, f32[]{:T(128)} %bitcast.86, f32[]{:T(128)S(6)} %sub.807, f32[]{:T(128)} %bitcast.85, ...), kind=kOutput, calls=%fused_computation.313 | convolution fusion | flops 50456576 | bytes 1049768 | tf_op jit(solution)/shard_map/ij,ojk->oik/dot_general | solution.py:75
  58.7 4.0 %convolution_bitcast_fusion = f32[1,32,4096]{2,1,0:T(8,128)S(1)} fusion(f32[4,8,32,128]{3,2,1,0:T(8,128)S(1)} %bitcast.285, f32[]{:T(128)} %bitcast.19, f32[]{:T(128)S(6)} %sub.758, f32[]{:T(128)} %bitcast.18, f32[]{:T(128)S(6)} %sub.756, f32[]{:T(128)} %bitcast.17, f32[]{:T(128)S(6)} %sub.754, f32[]{:T(128)} %bitcast.16, f32[]{:T(128)S(6)} %sub.752, ...), kind=kOutput, calls=%fused_computation | convolution fusion | flops 50456576 | bytes 1049768 | tf_op jit(solution)/shard_map/ij,ojk->oik/dot_general | solution.py:75
  67.5 5.6 %convolution_bitcast_fusion.6 = f32[1024,128]{0,1:T(8,128)S(1)} fusion(f32[1024,128]{1,0:T(8,128)S(1)} %bitcast.301, f32[]{:T(128)} %bitcast.54, f32[]{:T(128)S(6)} %sub.784, f32[]{:T(128)} %bitcast.53, f32[]{:T(128)S(6)} %sub.782, f32[]{:T(128)} %bitcast.52, f32[]{:T(128)S(6)} %sub.780, f32[]{:T(128)} %bitcast.51, f32[]{:T(128)S(6)} %sub.778, f32[]{:T(128)} %bitcast.50, ...), kind=kOutput, calls=%fused_computation.6 | convolution fusion | flops 204210176 | bytes 1055544 | tf_op jit(solution)/shard_map/dot_general | solution.py:65
  79.4 3.8 %fusion.119 = f32[32,128,32]{1,2,0:T(8,128)S(1)} fusion(f32[32,32,128]{2,1,0:T(8,128)S(1)} %bitcast.286, f32[]{:T(128)} %bitcast.62, f32[]{:T(128)S(6)} %sub.793, f32[]{:T(128)} %bitcast.61, f32[]{:T(128)S(6)} %sub.791, f32[]{:T(128)} %bitcast.60, f32[]{:T(128)S(6)} %sub.789, f32[]{:T(128)} %bitcast.59, f32[]{:T(128)S(6)} %sub.787, f32[]{:T(128)} %bitcast.58, ...), kind=kOutput, calls=%fused_computation.315 | convolution fusion | flops 50456576 | bytes 1049768 | tf_op jit(solution)/shard_map/ij,ojk->oik/dot_general | solution.py:75
  83.2 3.9 %convolution_bitcast_fusion.1 = f32[1,32,4096]{2,1,0:T(8,128)S(1)} fusion(f32[4,8,32,128]{3,2,1,0:T(8,128)S(1)} %bitcast.284, f32[]{:T(128)} %bitcast.69, f32[]{:T(128)S(6)} %sub.798, f32[]{:T(128)} %bitcast.68, f32[]{:T(128)S(6)} %sub.797, f32[]{:T(128)} %bitcast.67, f32[]{:T(128)S(6)} %sub.796, f32[]{:T(128)} %bitcast.66, f32[]{:T(128)S(6)} %sub.795, ...), kind=kOutput, calls=%fused_computation.1 | convolution fusion | flops 50456576 | bytes 1049768 | tf_op jit(solution)/shard_map/ij,ojk->oik/dot_general | solution.py:75
  89.5 16.8 %all-to-all-start = ((f32[64,1,4096]{2,1,0:T(1,128)}), f32[64,1,4096]{2,1,0:T(1,128)S(1)}, u32[]{:S(2)}, u32[]{:S(2)}) async-start(f32[64,1,4096]{2,1,0:T(1,128)} %all_to_all.32), calls=%async_computation | async-start | bytes 2097152 | tf_op jit(solution)/shard_map/all_to_all | solution.py:14
  117.2 2.7 pad_maximum_fusion.32
  123.1 2.7 pad_maximum_fusion.28
  148.5 4.5 %convolution_bitcast_fusion.5 = f32[8,8,16,128]{3,1,2,0:T(8,128)S(1)} fusion(f32[64,4096]{1,0:T(8,128)S(1)} %bitcast.292, f32[]{:T(128)} %bitcast.47, f32[]{:T(128)S(6)} %sub.771, f32[]{:T(128)} %bitcast.46, f32[]{:T(128)S(6)} %sub.770, f32[]{:T(128)} %bitcast.45, f32[]{:T(128)S(6)} %sub.769, f32[]{:T(128)} %bitcast.44, f32[]{:T(128)S(6)} %sub.768, ...), kind=kOutput, calls=%fused_computation.5 | convolution fusion | flops 101273600 | bytes 1063984 | tf_op jit(solution)/shard_map/dot_general | solution.py:86
  153.1 4.5 %convolution_bitcast_fusion.4 = f32[8,8,16,128]{3,1,2,0:T(8,128)S(1)} fusion(f32[64,4096]{1,0:T(8,128)S(1)} %bitcast.293, f32[]{:T(128)} %bitcast.25, f32[]{:T(128)S(6)} %sub.764, f32[]{:T(128)} %bitcast.24, f32[]{:T(128)S(6)} %sub.763, f32[]{:T(128)} %bitcast.23, f32[]{:T(128)S(6)} %sub.762, f32[]{:T(128)} %bitcast.22, f32[]{:T(128)S(6)} %sub.761, ...), kind=kOutput, calls=%fused_computation.4 | convolution fusion | flops 101273600 | bytes 1063984 | tf_op jit(solution)/shard_map/dot_general | solution.py:86
  157.8 5.6 %fusion.48 = f32[64,16,128]{2,1,0:T(8,128)S(1)} fusion(f32[64,16,128]{2,1,0:T(8,128)S(1)} %get-tuple-element.17, f32[]{:T(128)} %bitcast.54, f32[]{:T(128)S(6)} %sub.784, f32[]{:T(128)} %bitcast.53, f32[]{:T(128)S(6)} %sub.782, f32[]{:T(128)} %bitcast.52, f32[]{:T(128)S(6)} %sub.780, f32[]{:T(128)} %bitcast.51, f32[]{:T(128)S(6)} %sub.778, f32[]{:T(128)} %bitcast.50, ...), kind=kOutput, calls=%fused_computation.136 | convolution fusion | flops 204210176 | bytes 1055544 | tf_op jit(solution)/shard_map/dot_general | solution.py:65
  163.4 3.1 %fusion.199 = f32[64,128,16]{1,2,0:T(8,128)S(1)} fusion(f32[64,16,128]{2,1,0:T(8,128)S(1)} %fusion.48, f32[]{:T(128)} %bitcast.61, f32[]{:T(128)S(6)} %sub.791, f32[]{:T(128)} %bitcast.60, f32[]{:T(128)S(6)} %sub.789, f32[]{:T(128)} %bitcast.59, f32[]{:T(128)S(6)} %sub.787, f32[]{:T(128)} %bitcast.58, f32[]{:T(128)S(6)} %sub.785, ...), kind=kOutput, calls=%fused_computation.430 | convolution fusion | flops 25190144 | bytes 1049040 | tf_op jit(solution)/shard_map/ij,ojk->oik/dot_general | solution.py:75
  166.5 4.6 %convolution_bitcast_fusion.2 = f32[64,1,2048]{2,0,1:T(8,128)S(1)} fusion(f32[8,8,16,128]{3,2,1,0:T(8,128)S(1)} %bitcast.296, f32[]{:T(128)} %bitcast.47, f32[]{:T(128)S(6)} %sub.771, f32[]{:T(128)} %bitcast.46, f32[]{:T(128)S(6)} %sub.770, f32[]{:T(128)} %bitcast.45, f32[]{:T(128)S(6)} %sub.769, f32[]{:T(128)} %bitcast.44, f32[]{:T(128)S(6)} %sub.768, ...), kind=kOutput, calls=%fused_computation.2 | convolution fusion | flops 101273600 | bytes 1051504 | tf_op jit(solution)/shard_map/dot_general | solution.py:86
  172.4 12.5 %all-to-all-start.2 = ((f32[64,1,2048]{2,1,0:T(1,128)}), f32[64,1,2048]{2,1,0:T(1,128)S(1)}, u32[]{:S(2)}, u32[]{:S(2)}) async-start(f32[64,1,2048]{2,1,0:T(1,128)} %copy.18), calls=%async_computation.2 | async-start | bytes 1048576 | tf_op jit(solution)/shard_map/all_to_all | solution.py:178
  185.3 5.3 %fusion.50 = f32[64,16,128]{2,1,0:T(8,128)S(1)} fusion(f32[64,16,128]{2,1,0:T(8,128)S(1)} %get-tuple-element.18, f32[]{:T(128)} %bitcast.83, f32[]{:T(128)S(6)} %sub.805, f32[]{:T(128)} %bitcast.82, f32[]{:T(128)S(6)} %sub.804, f32[]{:T(128)} %bitcast.81, f32[]{:T(128)S(6)} %sub.803, f32[]{:T(128)} %bitcast.80, f32[]{:T(128)S(6)} %sub.802, f32[]{:T(128)} %bitcast.79, ...), kind=kOutput, calls=%fused_computation.138 | convolution fusion | flops 204210176 | bytes 1055544 | tf_op jit(solution)/shard_map/dot_general | solution.py:65
  190.6 3.1 %fusion.201 = f32[64,128,16]{1,2,0:T(8,128)S(1)} fusion(f32[64,16,128]{2,1,0:T(8,128)S(1)} %fusion.50, f32[]{:T(128)} %bitcast.88, f32[]{:T(128)S(6)} %sub.809, f32[]{:T(128)} %bitcast.87, f32[]{:T(128)S(6)} %sub.808, f32[]{:T(128)} %bitcast.86, f32[]{:T(128)S(6)} %sub.807, f32[]{:T(128)} %bitcast.85, f32[]{:T(128)S(6)} %sub.806, ...), kind=kOutput, calls=%fused_computation.432 | convolution fusion | flops 25190144 | bytes 1049040 | tf_op jit(solution)/shard_map/ij,ojk->oik/dot_general | solution.py:75
  193.7 4.6 %convolution_bitcast_fusion.3 = f32[64,1,2048]{2,0,1:T(8,128)S(1)} fusion(f32[8,8,16,128]{3,2,1,0:T(8,128)S(1)} %bitcast.295, f32[]{:T(128)} %bitcast.25, f32[]{:T(128)S(6)} %sub.764, f32[]{:T(128)} %bitcast.24, f32[]{:T(128)S(6)} %sub.763, f32[]{:T(128)} %bitcast.23, f32[]{:T(128)S(6)} %sub.762, f32[]{:T(128)} %bitcast.22, f32[]{:T(128)S(6)} %sub.761, ...), kind=kOutput, calls=%fused_computation.3 | convolution fusion | flops 101273600 | bytes 1051504 | tf_op jit(solution)/shard_map/dot_general | solution.py:86
  199.7 4.4 %all-to-all-done.2 = f32[64,1,2048]{2,1,0:T(1,128)S(1)} async-done(((f32[64,1,2048]{2,1,0:T(1,128)}), f32[64,1,2048]{2,1,0:T(1,128)S(1)}, u32[]{:S(2)}, u32[]{:S(2)}) %all-to-all-start.2) | async-done | bytes 524320 | tf_op jit(solution)/shard_map/all_to_all | solution.py:178
  204.0 8.6 %all-to-all-start.1 = ((f32[64,1,2048]{2,1,0:T(1,128)}), f32[64,1,2048]{2,1,0:T(1,128)S(1)}, u32[]{:S(2)}, u32[]{:S(2)}) async-start(f32[64,1,2048]{2,1,0:T(1,128)} %copy.17), calls=%async_computation.1 | async-start | bytes 1048576 | tf_op jit(solution)/shard_map/all_to_all | solution.py:177
  212.8 5.1 %fusion.390 = (f32[]{:T(128)}, f32[64,2048]{1,0:T(8,128)S(1)}) fusion(f32[64,1,2048]{2,1,0:T(1,128)S(1)} %all-to-all-done.2, f32[]{:T(128)} %bitcast.69, f32[]{:T(128)S(6)} %sub.798, f32[]{:T(128)} %bitcast.68, f32[]{:T(128)S(6)} %sub.797, f32[]{:T(128)} %bitcast.67, f32[]{:T(128)S(6)} %sub.796, f32[]{:T(128)} %bitcast.66, f32[]{:T(128)S(6)} %sub.795, ...), kind=kOutput, calls=%fused_computation.719 | convolution fusion | flops 101404672 | bytes 1051508 | tf_op jit(solution)/shard_map/dot_general | solution.py:86
  217.9 13.1 %all-to-all-done.1 = f32[64,1,2048]{2,1,0:T(1,128)S(1)} async-done(((f32[64,1,2048]{2,1,0:T(1,128)}), f32[64,1,2048]{2,1,0:T(1,128)S(1)}, u32[]{:S(2)}, u32[]{:S(2)}) %all-to-all-start.1) | async-done | bytes 524320 | tf_op jit(solution)/shard_map/all_to_all | solution.py:177
  231.0 5.2 %fusion.20 = (f32[]{:T(128)}, f32[64,2048]{1,0:T(8,128)S(1)}) fusion(f32[32,2048]{1,0:T(8,128)S(1)} %bitcast_multiply_fusion.4, f32[64]{0:T(128)S(1)} %mul.1305, f32[]{:T(128)S(6)} %mul.1081, f32[64,1,2048]{2,1,0:T(1,128)S(1)} %all-to-all-done.1, f32[]{:T(128)} %bitcast.19, f32[]{:T(128)S(6)} %sub.758, f32[]{:T(128)} %bitcast.18, f32[]{:T(128)S(6)} %sub.756, ...), kind=kOutput, calls=%fused_computation.32 | convolution fusion | flops 102060032 | bytes 1313912 | tf_op jit(solution)/shard_map/dot_general | solution.py:86
  238.2 4.9 %all-to-all-start.3 = ((f32[64,1,2]{2,1,0:T(1,128)}), f32[64,1,2]{2,1,0:T(1,128)S(1)}, u32[]{:S(2)}, u32[]{:S(2)}) async-start(f32[64,1,2]{2,1,0:T(1,128)} %broadcast_in_dim.646), calls=%async_computation.3 | async-start | bytes 65536 | tf_op jit(solution)/shard_map/all_to_all | solution.py:26
  244.9 10.2 %all-to-all-done.3 = f32[64,1,2]{2,1,0:T(1,128)S(1)} async-done(((f32[64,1,2]{2,1,0:T(1,128)}), f32[64,1,2]{2,1,0:T(1,128)S(1)}, u32[]{:S(2)}, u32[]{:S(2)}) %all-to-all-start.3) | async-done | bytes 544 | tf_op jit(solution)/shard_map/all_to_all | solution.py:26
  261.4 6.5 %collective-permute-done = f32[131072]{0:T(1024)S(1)} collective-permute-done((f32[131072]{0:T(1024)}, f32[131072]{0:T(1024)S(1)}, u32[]{:S(2)}, u32[]{:S(2)}) %collective-permute-start) | collective-permute-done | bytes 524320 | tf_op jit(solution)/shard_map/ppermute | solution.py:46
  270.0 4.6 %all-to-all-start.4 = ((f32[64,1,1]{2,1,0:T(1,128)}), f32[64,1,1]{2,1,0:T(1,128)S(1)}, u32[]{:S(2)}, u32[]{:S(2)}) async-start(f32[64,1,1]{2,1,0:T(1,128)} %broadcast_in_dim.647), calls=%async_computation.4 | async-start | bytes 65536 | tf_op jit(solution)/shard_map/all_to_all | solution.py:26
  276.5 10.0 %all-to-all-done.4 = f32[64,1,1]{2,1,0:T(1,128)S(1)} async-done(((f32[64,1,1]{2,1,0:T(1,128)}), f32[64,1,1]{2,1,0:T(1,128)S(1)}, u32[]{:S(2)}, u32[]{:S(2)}) %all-to-all-start.4) | async-done | bytes 288 | tf_op jit(solution)/shard_map/all_to_all | solution.py:26
  (186 shorter events, 62.2 us)
Async XLA Ops:
  0.8 0.7 copy-start.4
  3.7 0.7 copy-start.3
  25.3 24.1 %copy-start = (f32[1,131072]{1,0:T(1,128)S(1)}, f32[1,131072]{1,0:T(1,128)}, u32[]{:S(2)}) copy-start(f32[1,131072]{1,0:T(1,128)} %param.5) | copy-start | bytes 1572868
  62.7 4.8 %copy-start.1 = (f32[1,131072]{1,0:T(1,128)S(1)}, f32[1,131072]{1,0:T(1,128)}, u32[]{:S(2)}) copy-start(f32[1,131072]{1,0:T(1,128)} %param.4) | copy-start | bytes 1572868
  89.5 58.3 %all-to-all-start = ((f32[64,1,4096]{2,1,0:T(1,128)}), f32[64,1,4096]{2,1,0:T(1,128)S(1)}, u32[]{:S(2)}, u32[]{:S(2)}) async-start(f32[64,1,4096]{2,1,0:T(1,128)} %all_to_all.32), calls=%async_computation | async-start | bytes 2097152 | tf_op jit(solution)/shard_map/all_to_all | solution.py:14
  172.4 31.6 %all-to-all-start.2 = ((f32[64,1,2048]{2,1,0:T(1,128)}), f32[64,1,2048]{2,1,0:T(1,128)S(1)}, u32[]{:S(2)}, u32[]{:S(2)}) async-start(f32[64,1,2048]{2,1,0:T(1,128)} %copy.18), calls=%async_computation.2 | async-start | bytes 1048576 | tf_op jit(solution)/shard_map/all_to_all | solution.py:178
  204.0 27.0 %all-to-all-start.1 = ((f32[64,1,2048]{2,1,0:T(1,128)}), f32[64,1,2048]{2,1,0:T(1,128)S(1)}, u32[]{:S(2)}, u32[]{:S(2)}) async-start(f32[64,1,2048]{2,1,0:T(1,128)} %copy.17), calls=%async_computation.1 | async-start | bytes 1048576 | tf_op jit(solution)/shard_map/all_to_all | solution.py:177
  238.2 16.9 %all-to-all-start.3 = ((f32[64,1,2]{2,1,0:T(1,128)}), f32[64,1,2]{2,1,0:T(1,128)S(1)}, u32[]{:S(2)}, u32[]{:S(2)}) async-start(f32[64,1,2]{2,1,0:T(1,128)} %broadcast_in_dim.646), calls=%async_computation.3 | async-start | bytes 65536 | tf_op jit(solution)/shard_map/all_to_all | solution.py:26
  257.2 10.7 %collective-permute-start = (f32[131072]{0:T(1024)}, f32[131072]{0:T(1024)S(1)}, u32[]{:S(2)}, u32[]{:S(2)}) collective-permute-start(f32[131072]{0:T(1024)} %multiply_divide_fusion), channel_id=1, source_target_pairs={{0,64},{64,128},{128,192},{192,256},{256,320},{320,384},{384,448},... | collective-permute-start | bytes 1572872 | tf_op jit(solution)/shard_map/ppermute | solution.py:46
  261.3 6.6 %copy-start.2 = (f32[1,131072]{1,0:T(1,128)S(1)}, f32[1,131072]{1,0:T(1,128)}, u32[]{:S(2)}) copy-start(f32[1,131072]{1,0:T(1,128)} %param.4) | copy-start | bytes 1572868
  270.0 16.5 %all-to-all-start.4 = ((f32[64,1,1]{2,1,0:T(1,128)}), f32[64,1,1]{2,1,0:T(1,128)S(1)}, u32[]{:S(2)}, u32[]{:S(2)}) async-start(f32[64,1,1]{2,1,0:T(1,128)} %broadcast_in_dim.647), calls=%async_computation.4 | async-start | bytes 65536 | tf_op jit(solution)/shard_map/all_to_all | solution.py:26
where the time goes:
time: 291 us; the launch traced here: 289 us
  matrix products  71.8 us (25%)
  other arithmetic  54.3 us (19%)
  starting transfers between devices  49.3 us (17%)
  between operations  47 us (16%)
  waiting for transfers between devices  44.2 us (15%)
  local copies, waits for them, and re-layouts  22.1 us (8%)
    another operation x20, other arithmetic, bit_product(): pair = jnp.stack([anchor_zero[which], anchor_one[which]])  43.8 us
    dot_general x6, matrix products, mix_rows(): jnp.dot(kron_matrix(thetas_part), matrix, precision=lax.Precision.HIGHEST...  28.4 us
    dot_general x6, matrix products, mix_local(): jnp.einsum('ij,ojk->oik', kron_matrix(thetas_local[offset:offset + width_...  21.8 us
    dot_general x4, matrix products, mix_local(): jnp.dot(current, kron_matrix(thetas_local[:first_bits]), precision=lax.Pr...  21.7 us
    all_to_all x2, waiting for transfers between devices, copy_for_each(): return lax.all_to_all(copies, axis, split_axis=0, concat_axis=0, tiled=True)  20.2 us
    all_to_all x1, starting transfers between devices, side_by_side(): lax.all_to_all(both, axis, split_axis=split_dim, concat_axis=concat_dim,...  16.8 us
    all_to_all x1, waiting for transfers between devices, shards(): lax.all_to_all(fwd_part, 'state', split_axis=0, concat_axis=0, tiled=True)  13.1 us
    all_to_all x1, starting transfers between devices, shards(): lax.all_to_all(bwd_part, 'state', split_axis=0, concat_axis=0, tiled=True)  12.5 us
  transfers between devices with their start and end apart: 6, of which 5 were waited for; matrix products, arithmetic and copies ran while one was open for 18% of the time, Pallas kernels for 0%

commit v1 on v0

v1 whole, which is shorter than its diff:
```python
import jax
import jax.numpy as jnp
from jax import lax
from jax.experimental import pallas as pl
from jax.experimental.pallas import tpu as pltpu
from jax.sharding import PartitionSpec as P

PENALTY = 0.5
ERROR_RATE = 0.02
BASE_THETA = 0.01
LANE_BITS, LOW_BITS, SPLIT_BITS = 7, 11, 6
ROWS, LANES = 16, 128
MEIOSES = LOW_BITS + 2 * SPLIT_BITS
MID, HIGH = LOW_BITS, LOW_BITS + SPLIT_BITS
F32 = jnp.float32


def theta_list(theta_ref, marker):
    return [
        BASE_THETA * lax.shift_left(jnp.int32(1), theta_ref[marker, b]).astype(F32)
        for b in range(MEIOSES)
    ]


def anchor_list(mask_ref, marker):
    pairs = []
    for b in range(MEIOSES):
        mask = mask_ref[marker, b]
        zero = jnp.where(mask % 2 == 1, F32(1.0), F32(PENALTY))
        one = jnp.where(mask // 2 == 1, F32(1.0), F32(PENALTY))
        pairs.append((zero, one))
    return pairs


def lane_kron(thetas):
    differ = lax.broadcasted_iota(jnp.int32, (LANES, LANES), 0) ^ lax.broadcasted_iota(
        jnp.int32, (LANES, LANES), 1
    )
    result = jnp.ones((LANES, LANES), F32)
    for b in range(LANE_BITS):
        result = result * jnp.where((differ >> b) & 1 == 1, thetas[b], 1.0 - thetas[b])
    return result


def butterfly(values, thetas):
    values = list(values)
    for b, theta in enumerate(thetas):
        step = 1 << b
        for i in range(len(values)):
            if i & step == 0:
                moved = theta * (values[i + step] - values[i])
                values[i], values[i + step] = values[i] + moved, values[i + step] - moved
    return values


def mix_low(block, kron, thetas):
    block = jnp.dot(block, kron, precision=lax.Precision.HIGHEST, preferred_element_type=F32)
    block = block.reshape(-1, 8, LANES)
    row = lax.broadcasted_iota(jnp.int32, (1, 8, LANES), 1)
    for b in range(3):
        step = 1 << b
        other = pltpu.roll(block, step, axis=1)
        if step != 4:
            other = jnp.where((row >> b) & 1 == 1, other, pltpu.roll(block, 8 - step, axis=1))
        block = block + thetas[LANE_BITS + b] * (other - block)
    block = block.reshape(8, 2, 8, LANES)
    top, bottom = block[:, 0], block[:, 1]
    moved = thetas[10] * (bottom - top)
    top, bottom = top + moved, bottom - moved
    return [jnp.concatenate([top[j], bottom[j]], axis=0) for j in range(8)]


def low_factor(anchors):
    row = lax.broadcasted_iota(jnp.int32, (ROWS, LANES), 0)
    lane = lax.broadcasted_iota(jnp.int32, (ROWS, LANES), 1)
    position = row * LANES + lane
    result = jnp.full((ROWS, LANES), 1.0 - ERROR_RATE, F32)
    for b in range(LOW_BITS):
        zero, one = anchors[b]
        result = result * jnp.where((position >> b) & 1 == 1, one, zero)
    return result


def device_factor(anchors, first, device):
    result = F32(1.0)
    for b in range(SPLIT_BITS):
        zero, one = anchors[first + b]
        result = result * jnp.where((device >> b) & 1 == 1, one, zero)
    return result


def three_bits(anchors, first):
    factors = [None] * 8
    for i in range(8):
        value = anchors[first][i & 1]
        for b in (1, 2):
            value = value * anchors[first + b][(i >> b) & 1]
        factors[i] = value
    return factors


def emission_parts(mask_ref, marker, first_chunk, first_device, device):
    anchors = anchor_list(mask_ref, marker)
    own = device_factor(anchors, first_device, device)
    low = low_factor(anchors) * own
    inner = three_bits(anchors, first_chunk)
    outer = three_bits(anchors, first_chunk + 3)
    return outer, inner, low


def emitted(parts, i, j):
    outer, inner, low = parts
    return ERROR_RATE + (outer[i] * inner[j]) * low


def first_kernel(theta_ref, mask_ref, device_ref, fwd_ref, bwd_ref, out_ref, fwd_tmp, bwd_tmp):
    device = device_ref[0]
    for which, (source, tmp, marker) in enumerate(((fwd_ref, fwd_tmp, 0), (bwd_ref, bwd_tmp, 1))):
        thetas = theta_list(theta_ref, marker)
        kron = lane_kron(thetas)
        if which == 1:
            parts = emission_parts(mask_ref, 1, MID, HIGH, device)
        for i in range(8):
            block = source[pl.ds(i * 128, 128), :]
            if which == 1:
                block = jnp.concatenate(
                    [block[j * ROWS : (j + 1) * ROWS] * emitted(parts, i, j) for j in range(8)],
                    axis=0,
                )
            chunks = butterfly(mix_low(block, kron, thetas), thetas[MID : MID + 3])
            for j in range(8):
                tmp[8 * i + j] = chunks[j]
        for j in range(8):
            chunks = butterfly([tmp[8 * i + j] for i in range(8)], thetas[MID + 3 : HIGH])
            for i in range(8):
                out_ref[8 * i + j, pl.ds(which * ROWS, ROWS), :] = chunks[i]


def second_kernel(theta_ref, mask_ref, device_ref, in_ref, out_ref, tmp):
    device = device_ref[0]
    parts = emission_parts(mask_ref, 0, HIGH, MID, device)
    thetas = (theta_list(theta_ref, 0), theta_list(theta_ref, 1))
    kron = lane_kron(thetas[1])
    for which in range(2):
        before, after = thetas[which], thetas[1 - which]
        rows = pl.ds(which * ROWS, ROWS)
        for j in range(8):
            chunks = butterfly(
                [in_ref[8 * i + j, rows, :] for i in range(8)], before[HIGH + 3 : MEIOSES]
            )
            for i in range(8):
                tmp[8 * i + j] = chunks[i]
        for i in range(8):
            chunks = butterfly([tmp[8 * i + j] for j in range(8)], before[HIGH : HIGH + 3])
            chunks = [chunks[j] * emitted(parts, i, j) for j in range(8)]
            chunks = butterfly(chunks, after[HIGH : HIGH + 3])
            if which == 0:
                chunks = mix_low(jnp.concatenate(chunks, axis=0), kron, after)
            for j in range(8):
                tmp[8 * i + j] = chunks[j]
        for j in range(8):
            chunks = butterfly([tmp[8 * i + j] for i in range(8)], after[HIGH + 3 : MEIOSES])
            for i in range(8):
                out_ref[8 * i + j, rows, :] = chunks[i]


def forward_kernel(theta_ref, mask_ref, device_ref, in_ref, out_ref, sum_ref, tmp):
    device = device_ref[0]
    parts = emission_parts(mask_ref, 1, MID, HIGH, device)
    thetas = theta_list(theta_ref, 1)
    for i in range(8):
        chunks = butterfly(
            [in_ref[8 * i + j, pl.ds(0, ROWS), :] for j in range(8)], thetas[MID : MID + 3]
        )
        for j in range(8):
            tmp[8 * i + j] = chunks[j]
    acc = jnp.zeros((ROWS, LANES), F32)
    for j in range(8):
        chunks = butterfly([tmp[8 * i + j] for i in range(8)], thetas[MID + 3 : HIGH])
        for i in range(8):
            value = chunks[i] * emitted(parts, i, j)
            acc = acc + value
            out_ref[pl.ds((8 * i + j) * ROWS, ROWS), :] = value
    sum_ref[...] = acc[:8] + acc[8:]


def backward_kernel(theta_ref, in_ref, out_ref, sum_ref, tmp):
    thetas = theta_list(theta_ref, 0)
    kron = lane_kron(thetas)
    for i in range(8):
        block = jnp.concatenate(
            [in_ref[8 * i + j, pl.ds(ROWS, ROWS), :] for j in range(8)], axis=0
        )
        chunks = butterfly(mix_low(block, kron, thetas), thetas[MID : MID + 3])
        for j in range(8):
            tmp[8 * i + j] = chunks[j]
    acc = jnp.zeros((ROWS, LANES), F32)
    for j in range(8):
        chunks = butterfly([tmp[8 * i + j] for i in range(8)], thetas[MID + 3 : HIGH])
        for i in range(8):
            acc = acc + chunks[i]
            out_ref[pl.ds((8 * i + j) * ROWS, ROWS), :] = chunks[i]
    sum_ref[...] = acc[:8] + acc[8:]


def product_kernel(seg_ref, first_ref, got_ref, bwd_ref, fsum_ref, bsum_ref, out_ref, sum_ref):
    acc = jnp.zeros((8, LANES), F32)
    is_first = seg_ref[0] == 0
    for i in range(16):
        rows = pl.ds(64 * i, 64)
        left = jnp.where(is_first, first_ref[rows, :], got_ref[rows, :])
        value = left * bwd_ref[rows, :]
        out_ref[rows, :] = value
        acc = acc + jnp.sum(value.reshape(8, 8, LANES), axis=0)
    lane = lax.broadcasted_iota(jnp.int32, (1, LANES), 1)
    row = jnp.where(
        lane == 0,
        jnp.sum(fsum_ref[...]),
        jnp.where(lane == 1, jnp.sum(bsum_ref[...]), jnp.sum(acc)),
    )
    sum_ref[...] = jnp.broadcast_to(row[None], sum_ref.shape)


def scale_kernel(total_ref, fwd_ref, bwd_ref, post_ref, fwd_out, bwd_out, post_out, log_ref):
    totals = jnp.sum(total_ref[...], axis=0)
    means = totals * (1.0 / 2.0**MEIOSES)
    lane = lax.broadcasted_iota(jnp.int32, (1, LANES), 1)
    for which, (source, target) in enumerate(
        ((fwd_ref, fwd_out), (bwd_ref, bwd_out), (post_ref, post_out))
    ):
        mean = jnp.sum(jnp.where(lane == which, means, 0.0), axis=1, keepdims=True)
        scale = 1.0 / mean
        for i in range(8):
            rows = pl.ds(128 * i, 128)
            target[rows, :] = source[rows, :] * scale
        if which < 2:
            log_ref[pl.ds(which, 1), :] = jnp.log(mean)


SMEM = pl.BlockSpec(memory_space=pltpu.SMEM)
VMEM = pl.BlockSpec(memory_space=pltpu.VMEM)


def call(kernel, name, n_scalar, n_vector, outs, scratch=()):
    return pl.pallas_call(
        kernel,
        name=name,
        in_specs=[SMEM] * n_scalar + [VMEM] * n_vector,
        out_specs=[VMEM] * len(outs),
        out_shape=[jax.ShapeDtypeStruct(o, F32) for o in outs],
        scratch_shapes=[pltpu.VMEM(s, F32) for s in scratch],
    )


def exchanged(blocks):
    return lax.all_to_all(blocks, "state", split_axis=0, concat_axis=0, tiled=True)


def shards(forward_in, backward_in, compat_masks, theta_index):
    groups = lax.axis_size("state")
    chunk = (groups, ROWS, LANES)
    pair = (groups, 2 * ROWS, LANES)
    flat = (groups * ROWS, LANES)
    device = lax.axis_index("state").reshape(1)
    seg = lax.axis_index("seg").reshape(1)
    first = forward_in.reshape(flat)
    (both,) = call(first_kernel, "first", 3, 2, [pair], [chunk, chunk])(
        theta_index, compat_masks, device, first, backward_in.reshape(flat)
    )
    both = exchanged(both)
    (both,) = call(second_kernel, "second", 3, 1, [pair], [chunk])(
        theta_index, compat_masks, device, both
    )
    both = exchanged(both)
    forward, fsum = call(forward_kernel, "forward", 3, 1, [flat, (8, LANES)], [chunk])(
        theta_index, compat_masks, device, both
    )
    count = lax.axis_size("seg")
    received = lax.ppermute(forward, "seg", [(s, s + 1) for s in range(count - 1)])
    backward, bsum = call(backward_kernel, "backward", 1, 1, [flat, (8, LANES)], [chunk])(
        theta_index, both
    )
    product, sums = call(product_kernel, "product", 1, 5, [flat, (groups, 1, LANES)])(
        seg, first, received, backward, fsum, bsum
    )
    totals = exchanged(sums)
    forward, backward, posterior, logs = call(
        scale_kernel, "scale", 0, 4, [flat, flat, flat, (2, 1)]
    )(totals, forward, backward, product)
    return forward.reshape(1, -1), backward.reshape(1, -1), posterior.reshape(1, -1), logs


def solution(mesh):
    placed = (P("seg", "state"), P("seg", "state"), P("seg", None), P("seg", None))
    return jax.shard_map(
        shards,
        mesh=mesh,
        in_specs=placed,
        out_specs=(P("seg", "state"), P("seg", "state"), P("seg", "state"), P(None, "seg")),
        check_vma=False,
    )
```

time: 291 us -> 130 us (0.45)
  blocking collectives: 0 us -> 100 us
  matrix products: 71.8 us -> 0 us
  other arithmetic: 54.3 us -> 0 us
  starting transfers between devices: 49.3 us -> 1.91 us
  between operations: 47 us -> 0.66 us
  waiting for transfers between devices: 44.2 us -> 5.77 us
  local copies, waits for them, and re-layouts: 22.1 us -> 2.05 us
  Pallas kernels: 0 us -> 18.6 us
    all_to_all x0 -> x3, blocking collectives: none -> 100 us  [exchanged(): lax.all_to_all(blocks, 'state', split_axis=0, concat_axis=0, tiled=True)]
    dot_general x16 -> x0, matrix products: 71.8 us -> none  [the longest x6 28.4 us: mix_rows(): jnp.dot(kron_matrix(thetas_part), matrix, precision=lax.Precision.HIGHEST...]
    all_to_all x5 -> x0, starting transfers between devices: 47.4 us -> none  [the longest x1 16.8 us: side_by_side(): lax.all_to_all(both, axis, split_axis=split_dim, concat_axis=concat_dim,...]
    another operation x20 -> x0, other arithmetic: 43.8 us -> none  [bit_product(): pair = jnp.stack([anchor_zero[which], anchor_one[which]])]
    all_to_all x5 -> x0, waiting for transfers between devices: 37.7 us -> none  [the longest x2 20.2 us: copy_for_each(): return lax.all_to_all(copies, axis, split_axis=0, concat_axis=0, tiled=True)]
    pallas_call x0 -> x6, Pallas kernels: none -> 18.6 us  [the longest x1 4.14 us: shards(): call(first_kernel, 'first', 3, 2, [pair], [chunk, chunk])]
    slice x10 -> x0, local copies, waits for them, and re-layouts: 6.91 us -> none  [the longest x6 4.2 us: bit_product(): pair = jnp.stack([anchor_zero[which], anchor_one[which]])]
    all_to_all x3 -> x0, local copies, waits for them, and re-layouts: 4.86 us -> none  [the longest x1 2.19 us: side_by_side(): lax.all_to_all(both, axis, split_axis=split_dim, concat_axis=concat_dim,...]
  transfers between devices with their start and end apart: 6 -> 1, of which waited for: 5 -> 1; matrix products, arithmetic and copies ran while one was open for 18% -> 0% of each run, Pallas kernels for 0% -> 2%
where the time goes in v1:
time: 130 us; the launch traced here: 129 us
  blocking collectives  100 us (77%)
  Pallas kernels  18.6 us (14%)
  waiting for transfers between devices  5.77 us (4%)
  local copies, waits for them, and re-layouts  2.05 us (2%)
  starting transfers between devices  1.91 us (1%)
    all_to_all x3, blocking collectives, exchanged(): lax.all_to_all(blocks, 'state', split_axis=0, concat_axis=0, tiled=True)  100 us
    ppermute x1, waiting for transfers between devices, shards(): lax.ppermute(forward, 'seg', [(s, s + 1) for s in range(count - 1)])  5.77 us
    pallas_call x1, Pallas kernels, shards(): call(first_kernel, 'first', 3, 2, [pair], [chunk, chunk])  4.14 us
    pallas_call x1, Pallas kernels, shards(): call(second_kernel, 'second', 3, 1, [pair], [chunk])  4.02 us
    pallas_call x1, Pallas kernels, shards(): call(backward_kernel, 'backward', 1, 1, [flat, (8, LANES)], [chunk])  3.01 us
    pallas_call x1, Pallas kernels, shards(): call(scale_kernel, 'scale', 0, 4, [flat, flat, flat, (2, 1)])  2.7 us
  transfers between devices with their start and end apart: 1, of which 1 were waited for; matrix products, arithmetic and copies ran while one was open for 0% of the time, Pallas kernels for 2%

profile of v1, /device:TPU:6, one launch (start us, length us, event | category | flops | bytes accessed | tf_op | source)
XLA Modules:
  0.0 129.2 jit_solution(18175123330826940176)
XLA Ops:
  0.6 4.1 %first.1 = f32[64,32,128]{2,1,0:T(8,128)} custom-call(s32[2,23]{1,0:T(2,128)} %theta_ref.7, s32[2,23]{1,0:T(2,128)} %mask_ref.5, s32[1]{0:T(128)} %bitcast.2.device_ref, f32[1024,128]{1,0:T(8,128)} %bitcast.7, f32[1024,128]{1,0:T(8,128)} %bitcast.9), custom_call_target="tpu_custom_call" | custom-call | tf_op jit(solution)/shard_map/first/pallas_call | solution.py:267
  4.8 46.4 %all_to_all.15.in_ref = f32[64,32,128]{2,1,0:T(8,128)} all-to-all(f32[64,32,128]{2,1,0:T(8,128)} %first.1), channel_id=1, replica_groups=mesh['seg'=8,'state'=64] {'state'}, dimensions={0} | all-to-all | bytes 2097152 | tf_op jit(solution)/shard_map/all_to_all | solution.py:256
  51.2 4.0 %second.1 = f32[64,32,128]{2,1,0:T(8,128)} custom-call(s32[2,23]{1,0:T(2,128)} %theta_ref.7, s32[2,23]{1,0:T(2,128)} %mask_ref.5, s32[1]{0:T(128)} %bitcast.2.device_ref, f32[64,32,128]{2,1,0:T(8,128)} %all_to_all.15.in_ref), custom_call_target="tpu_custom_call" | custom-call | tf_op jit(solution)/shard_map/second/pallas_call | solution.py:271
  55.2 35.5 %all_to_all.16.in_ref = f32[64,32,128]{2,1,0:T(8,128)} all-to-all(f32[64,32,128]{2,1,0:T(8,128)} %second.1), channel_id=1, replica_groups=mesh['seg'=8,'state'=64] {'state'}, dimensions={0} | all-to-all | bytes 2097152 | tf_op jit(solution)/shard_map/all_to_all | solution.py:256
  90.7 2.5 %forward.1 = (f32[1024,128]{1,0:T(8,128)}, f32[8,128]{1,0:T(8,128)}) custom-call(s32[2,23]{1,0:T(2,128)} %theta_ref.7, s32[2,23]{1,0:T(2,128)} %mask_ref.5, s32[1]{0:T(128)} %bitcast.2.device_ref, f32[64,32,128]{2,1,0:T(8,128)} %all_to_all.16.in_ref), custom_call_target="tpu_custom_call" | custom-call | tf_op jit(solution)/shard_map/forward/pallas_call | solution.py:275
  93.2 1.9 %collective-permute-start = (f32[1024,128]{1,0:T(8,128)}, f32[1024,128]{1,0:T(8,128)S(1)}, u32[]{:S(2)}, u32[]{:S(2)}) collective-permute-start(f32[1024,128]{1,0:T(8,128)} %get-tuple-element.14.fwd_ref), channel_id=1, source_target_pairs={{0,64},{64,128},{128,192},{192,256},{256,320},{320,384},{384,448},... | collective-permute-start | bytes 1572872 | tf_op jit(solution)/shard_map/ppermute | solution.py:279
  95.2 3.0 %backward.1 = (f32[1024,128]{1,0:T(8,128)}, f32[8,128]{1,0:T(8,128)}) custom-call(s32[2,23]{1,0:T(2,128)} %theta_ref.7, f32[64,32,128]{2,1,0:T(8,128)} %all_to_all.16.in_ref), custom_call_target="tpu_custom_call" | custom-call | tf_op jit(solution)/shard_map/backward/pallas_call | solution.py:280
  98.2 5.8 %collective-permute-done.got_ref = f32[1024,128]{1,0:T(8,128)S(1)} collective-permute-done((f32[1024,128]{1,0:T(8,128)}, f32[1024,128]{1,0:T(8,128)S(1)}, u32[]{:S(2)}, u32[]{:S(2)}) %collective-permute-start) | collective-permute-done | bytes 524320 | tf_op jit(solution)/shard_map/ppermute | solution.py:279
  103.9 0.0 copy-start
  103.9 0.8 copy-done
  104.7 2.2 %product.1 = (f32[1024,128]{1,0:T(8,128)}, f32[64,1,128]{2,1,0:T(1,128)}) custom-call(s32[1]{0:T(128)} %bitcast.seg_ref, f32[1024,128]{1,0:T(8,128)} %bitcast.8, f32[1024,128]{1,0:T(8,128)} %copy-done, f32[1024,128]{1,0:T(8,128)} %get-tuple-element.15.bwd_ref, f32[8,128]{1,0:T(8,128)} %get-tuple-element.16.fsum_ref, f32[8,128]{1,0:T(8,128)} %get-tuple-element.17.bsum_ref), custom_call_target="tpu_custom_call" | custom-call | tf_op jit(solution)/shard_map/product/pallas_call | solution.py:283
  107.0 18.3 %all_to_all.17.total_ref = f32[64,1,128]{2,1,0:T(1,128)} all-to-all(f32[64,1,128]{2,1,0:T(1,128)} %get-tuple-element.18), channel_id=1, replica_groups=mesh['seg'=8,'state'=64] {'state'}, dimensions={0} | all-to-all | bytes 65536 | tf_op jit(solution)/shard_map/all_to_all | solution.py:256
  125.2 2.7 %scale.1 = (f32[1024,128]{1,0:T(8,128)}, f32[1024,128]{1,0:T(8,128)}, f32[1024,128]{1,0:T(8,128)}, f32[2,1]{1,0:T(2,128)}) custom-call(f32[64,1,128]{2,1,0:T(1,128)} %all_to_all.17.total_ref, f32[1024,128]{1,0:T(8,128)} %get-tuple-element.14.fwd_ref, f32[1024,128]{1,0:T(8,128)} %get-tuple-element.15.bwd_ref, f32[1024,128]{1,0:T(8,128)} %get-tuple-element.19.post_ref), custom_call_target="tpu_custom_call" | custom-call | tf_op jit(solution)/shard_map/scale/pallas_call | solution.py:287
  127.9 0.0 copy-start.1
  127.9 0.7 copy-done.1
  128.6 0.6 copy.8
Async XLA Ops:
  93.2 10.7 %collective-permute-start = (f32[1024,128]{1,0:T(8,128)}, f32[1024,128]{1,0:T(8,128)S(1)}, u32[]{:S(2)}, u32[]{:S(2)}) collective-permute-start(f32[1024,128]{1,0:T(8,128)} %get-tuple-element.14.fwd_ref), channel_id=1, source_target_pairs={{0,64},{64,128},{128,192},{192,256},{256,320},{320,384},{384,448},... | collective-permute-start | bytes 1572872 | tf_op jit(solution)/shard_map/ppermute | solution.py:279
  103.9 0.8 copy-start
  127.9 0.7 copy-start.1

commit v2 on v1

v2 whole, which is shorter than its diff:
```python
import jax
import jax.numpy as jnp
from jax import lax
from jax.experimental import pallas as pl
from jax.experimental.pallas import tpu as pltpu
from jax.sharding import PartitionSpec as P

PENALTY = 0.5
ERROR_RATE = 0.02
BASE_THETA = 0.01
LANE_BITS, LOW_BITS, SPLIT_BITS = 7, 11, 6
ROWS, LANES = 16, 128
MEIOSES = LOW_BITS + 2 * SPLIT_BITS
MID, HIGH = LOW_BITS, LOW_BITS + SPLIT_BITS
F32, BF16 = jnp.float32, jnp.bfloat16


def theta_list(theta_ref, marker):
    return [
        BASE_THETA * lax.shift_left(jnp.int32(1), theta_ref[marker, b]).astype(F32)
        for b in range(MEIOSES)
    ]


def anchor_list(mask_ref, marker):
    pairs = []
    for b in range(MEIOSES):
        mask = mask_ref[marker, b]
        zero = jnp.where(mask % 2 == 1, F32(1.0), F32(PENALTY))
        one = jnp.where(mask // 2 == 1, F32(1.0), F32(PENALTY))
        pairs.append((zero, one))
    return pairs


def kron_rows(thetas):
    row = lax.broadcasted_iota(jnp.int32, (8, LANES), 0)
    lane = lax.broadcasted_iota(jnp.int32, (8, LANES), 1)
    low = jnp.ones((8, LANES), F32)
    for b in range(3):
        low = low * jnp.where(((row ^ lane) >> b) & 1 == 1, thetas[b], 1.0 - thetas[b])
    pieces = [low]
    for b in range(3, 7):
        bit = (lane >> b) & 1 == 1
        same = jnp.where(bit, thetas[b], 1.0 - thetas[b])
        other = jnp.where(bit, 1.0 - thetas[b], thetas[b])
        pieces = [p * same for p in pieces] + [p * other for p in pieces]
    return jnp.concatenate(pieces, axis=0)


def two_parts(x):
    high = x.astype(BF16)
    return high, (x - high.astype(F32)).astype(BF16)


def mix_lanes(x, kron):
    high, low = two_parts(x)
    left = jnp.concatenate([high, low, high, low], axis=1)
    right = jnp.concatenate([kron[0], kron[0], kron[1], kron[1]], axis=0)
    return jnp.dot(left, right, preferred_element_type=F32)


def mix_row_bits(kron, x):
    high, low = two_parts(x)
    left = jnp.concatenate([kron[0], kron[0], kron[1], kron[1]], axis=1)
    right = jnp.concatenate([high, low, high, low], axis=0)
    return jnp.dot(left, right, preferred_element_type=F32)


def mix_blocks(chunks, lanes, rows):
    mixed = mix_lanes(jnp.concatenate(chunks, axis=0), lanes)
    mixed = mix_row_bits(rows, jnp.concatenate([mixed[:128], mixed[128:]], axis=1))
    return [
        mixed[j * ROWS : (j + 1) * ROWS, half * LANES : (half + 1) * LANES]
        for half in range(2)
        for j in range(8)
    ]


def butterfly(values, thetas):
    values = list(values)
    for b, theta in enumerate(thetas):
        step = 1 << b
        for i in range(len(values)):
            if i & step == 0:
                moved = theta * (values[i + step] - values[i])
                values[i], values[i + step] = values[i] + moved, values[i + step] - moved
    return values


def low_factor(anchors):
    row = lax.broadcasted_iota(jnp.int32, (ROWS, LANES), 0)
    lane = lax.broadcasted_iota(jnp.int32, (ROWS, LANES), 1)
    position = row * LANES + lane
    result = jnp.full((ROWS, LANES), 1.0 - ERROR_RATE, F32)
    for b in range(LOW_BITS):
        zero, one = anchors[b]
        result = result * jnp.where((position >> b) & 1 == 1, one, zero)
    return result


def device_factor(anchors, first, device):
    result = F32(1.0)
    for b in range(SPLIT_BITS):
        zero, one = anchors[first + b]
        result = result * jnp.where((device >> b) & 1 == 1, one, zero)
    return result


def three_bits(anchors, first):
    factors = [None] * 8
    for i in range(8):
        value = anchors[first][i & 1]
        for b in (1, 2):
            value = value * anchors[first + b][(i >> b) & 1]
        factors[i] = value
    return factors


def low_table(anchors, first_device, device):
    return low_factor(anchors) * device_factor(anchors, first_device, device)


THETAS, FACTORS, TABLE = 0, 64, 128


def table_thetas(table_ref, marker):
    return [table_ref[THETAS + 32 * marker + b] for b in range(MEIOSES)]


def emitted(table_ref, low_ref, layout, i, j):
    scalar = table_ref[FACTORS + 16 * layout + i] * table_ref[FACTORS + 16 * layout + 8 + j]
    return ERROR_RATE + scalar * low_ref[layout]


def first_kernel(theta_ref, mask_ref, device_ref, fwd_ref, bwd_ref, out_ref, table_ref, low_ref, kron_ref, rows_ref,
                 fwd_in, bwd_in, tmp, sems):
    copies = [
        [
            pltpu.make_async_copy(
                source.at[pl.ds(p * 256, 256), :], target.at[pl.ds(p * 256, 256), :], sems.at[which, p]
            )
            for p in range(4)
        ]
        for which, (source, target) in enumerate(((fwd_ref, fwd_in), (bwd_ref, bwd_in)))
    ]
    for row in copies:
        for copy in row:
            copy.start()
    device = device_ref[0]
    thetas = [theta_list(theta_ref, m) for m in range(2)]
    for m in range(2):
        for b in range(MEIOSES):
            table_ref[THETAS + 32 * m + b] = thetas[m][b]
    for layout, (marker, chunk, own) in enumerate(((0, HIGH, MID), (1, MID, HIGH))):
        anchors = anchor_list(mask_ref, marker)
        low_ref[layout] = low_table(anchors, own, device)
        for at, bits in ((0, chunk + 3), (8, chunk)):
            for i, value in enumerate(three_bits(anchors, bits)):
                table_ref[FACTORS + 16 * layout + at + i] = value
    for m in range(2):
        for part, value in enumerate(two_parts(kron_rows(thetas[m][:7]))):
            kron_ref[m, part] = value
        for part, value in enumerate(two_parts(kron_rows(thetas[m][7:14]))):
            rows_ref[m, part] = value
    for part, value in enumerate(two_parts(kron_rows(thetas[1][7:11] + thetas[1][17:20]))):
        rows_ref[2, part] = value
    for which, source in enumerate((fwd_in, bwd_in)):
        for p in range(4):
            copies[which][p].wait()
            chunks = [source[pl.ds(p * 256 + k * ROWS, ROWS), :] for k in range(16)]
            if which == 1:
                chunks = [
                    chunks[k] * emitted(table_ref, low_ref, 1, 2 * p + k // 8, k % 8)
                    for k in range(16)
                ]
            chunks = mix_blocks(chunks, kron_ref[which], rows_ref[which])
            for k in range(16):
                tmp[which, 16 * p + k] = chunks[k]
        for j in range(8):
            chunks = butterfly([tmp[which, 8 * i + j] for i in range(8)], thetas[which][14:17])
            for i in range(8):
                out_ref[8 * i + j, pl.ds(which * ROWS, ROWS), :] = chunks[i]


def second_kernel(table_ref, in_ref, low_ref, kron_ref, rows_ref, out_ref, tmp):
    thetas = [table_thetas(table_ref, m) for m in range(2)]
    for which in range(2):
        before, after = thetas[which], thetas[1 - which]
        rows = pl.ds(which * ROWS, ROWS)
        for j in range(8):
            chunks = butterfly([in_ref[8 * i + j, rows, :] for i in range(8)], before[20:23])
            for i in range(8):
                tmp[which, 8 * i + j] = chunks[i]
        for pair in range(4):
            both = []
            for i in (2 * pair, 2 * pair + 1):
                chunks = butterfly([tmp[which, 8 * i + j] for j in range(8)], before[17:20])
                chunks = [chunks[j] * emitted(table_ref, low_ref, 0, i, j) for j in range(8)]
                if which == 1:
                    chunks = butterfly(chunks, after[17:20])
                both += chunks
            if which == 0:
                both = mix_blocks(both, kron_ref[1], rows_ref[2])
            for k in range(16):
                tmp[which, 16 * pair + k] = both[k]
        for j in range(8):
            chunks = butterfly([tmp[which, 8 * i + j] for i in range(8)], after[20:23])
            for i in range(8):
                out_ref[8 * i + j, rows, :] = chunks[i]


def forward_kernel(table_ref, in_ref, low_ref, out_ref, sum_ref, tmp):
    thetas = table_thetas(table_ref, 1)
    for i in range(8):
        chunks = butterfly([in_ref[8 * i + j, pl.ds(0, ROWS), :] for j in range(8)], thetas[11:14])
        for j in range(8):
            tmp[8 * i + j] = chunks[j]
    acc = jnp.zeros((ROWS, LANES), F32)
    for j in range(8):
        chunks = butterfly([tmp[8 * i + j] for i in range(8)], thetas[14:17])
        for i in range(8):
            value = chunks[i] * emitted(table_ref, low_ref, 1, i, j)
            acc = acc + value
            out_ref[pl.ds((8 * i + j) * ROWS, ROWS), :] = value
    sum_ref[...] = acc[:8] + acc[8:]


def backward_kernel(table_ref, in_ref, kron_ref, rows_ref, out_ref, sum_ref, tmp):
    thetas = table_thetas(table_ref, 0)
    for p in range(4):
        chunks = [in_ref[16 * p + k, pl.ds(ROWS, ROWS), :] for k in range(16)]
        chunks = mix_blocks(chunks, kron_ref[0], rows_ref[0])
        for k in range(16):
            tmp[16 * p + k] = chunks[k]
    acc = jnp.zeros((ROWS, LANES), F32)
    for j in range(8):
        chunks = butterfly([tmp[8 * i + j] for i in range(8)], thetas[14:17])
        for i in range(8):
            acc = acc + chunks[i]
            out_ref[pl.ds((8 * i + j) * ROWS, ROWS), :] = chunks[i]
    sum_ref[...] = acc[:8] + acc[8:]


def product_kernel(seg_ref, got_ref, bwd_ref, fsum_ref, bsum_ref, first_ref, out_ref, sum_ref, first_in, sem):
    is_first = seg_ref[0] == 0

    @pl.when(is_first)
    def _():
        copy = pltpu.make_async_copy(first_ref, first_in, sem)
        copy.start()
        copy.wait()

    def multiply(left_ref):
        acc = jnp.zeros((8, LANES), F32)
        for i in range(16):
            rows = pl.ds(64 * i, 64)
            value = left_ref[rows, :] * bwd_ref[rows, :]
            out_ref[rows, :] = value
            acc = acc + jnp.sum(value.reshape(8, 8, LANES), axis=0)
        lane = lax.broadcasted_iota(jnp.int32, (1, LANES), 1)
        row = jnp.where(
            lane == 0,
            jnp.sum(fsum_ref[...]),
            jnp.where(lane == 1, jnp.sum(bsum_ref[...]), jnp.sum(acc)),
        )
        sum_ref[...] = jnp.broadcast_to(row[None], sum_ref.shape)

    pl.when(is_first)(lambda: multiply(first_in))
    pl.when(jnp.logical_not(is_first))(lambda: multiply(got_ref))


def scale_kernel(total_ref, fwd_ref, bwd_ref, post_ref, fwd_out, bwd_out, post_out, log_ref, ready, sems):
    totals = jnp.sum(total_ref[...], axis=0)
    means = totals * (1.0 / 2.0**MEIOSES)
    lane = lax.broadcasted_iota(jnp.int32, (1, LANES), 1)
    copies = []
    for which, (source, target) in enumerate(
        ((fwd_ref, fwd_out), (bwd_ref, bwd_out), (post_ref, post_out))
    ):
        mean = jnp.sum(jnp.where(lane == which, means, 0.0), axis=1, keepdims=True)
        scale = 1.0 / mean
        for half in range(2):
            for i in range(4):
                rows = pl.ds(half * 512 + 128 * i, 128)
                ready[which, rows, :] = source[rows, :] * scale
            rows = pl.ds(half * 512, 512)
            copy = pltpu.make_async_copy(
                ready.at[which, rows, :], target.at[rows, :], sems.at[which, half]
            )
            copy.start()
            copies.append(copy)
        if which < 2:
            log_ref[:, pl.ds(which, 1)] = jnp.log(mean)
    for copy in copies:
        copy.wait()


SMEM = pl.BlockSpec(memory_space=pltpu.SMEM)
VMEM = pl.BlockSpec(memory_space=pltpu.VMEM)
ANY = pl.BlockSpec(memory_space=pl.ANY)


def kept(array):
    return pltpu.with_memory_space_constraint(array, pltpu.VMEM)


def vmem(*shape, dtype=F32):
    return (VMEM, pltpu.VMEM(shape, dtype))


def exchanged(blocks):
    return lax.all_to_all(blocks, "state", split_axis=0, concat_axis=0, tiled=True)


def call(kernel, name, scalars, vectors, raw, outs, scratch=()):
    return pl.pallas_call(
        kernel,
        name=name,
        in_specs=[SMEM] * len(scalars) + [VMEM] * len(vectors) + [ANY] * len(raw),
        out_specs=[o[0] for o in outs],
        out_shape=[o[1] for o in outs],
        scratch_shapes=scratch,
    )(*scalars, *[kept(v) for v in vectors], *raw)


def shards(forward_in, backward_in, compat_masks, theta_index):
    groups = lax.axis_size("state")
    pair = (groups, 2 * ROWS, LANES)
    flat = (groups * ROWS, LANES)
    chunk = (groups, ROWS, LANES)
    device = lax.axis_index("state").reshape(1)
    seg = lax.axis_index("seg").reshape(1)
    first = forward_in.reshape(flat)
    both, table, low, kron, rows = call(
        first_kernel,
        "first",
        (theta_index, compat_masks, device),
        (),
        (first, backward_in.reshape(flat)),
        [
            vmem(*pair),
            (SMEM, jax.ShapeDtypeStruct((TABLE,), F32)),
            vmem(2, ROWS, LANES),
            vmem(2, 2, LANES, LANES, dtype=BF16),
            vmem(3, 2, LANES, LANES, dtype=BF16),
        ],
        [
            pltpu.VMEM(flat, F32),
            pltpu.VMEM(flat, F32),
            pltpu.VMEM((2, *chunk), F32),
            pltpu.SemaphoreType.DMA((2, 4)),
        ],
    )
    both = exchanged(both)
    (both,) = call(
        second_kernel,
        "second",
        (table,),
        (both, low, kron, rows),
        (),
        [vmem(*pair)],
        [pltpu.VMEM((2, *chunk), F32)],
    )
    both = exchanged(both)
    forward, fsum = call(
        forward_kernel,
        "forward",
        (table,),
        (both, low),
        (),
        [vmem(*flat), vmem(8, LANES)],
        [pltpu.VMEM(chunk, F32)],
    )
    count = lax.axis_size("seg")
    received = lax.ppermute(forward, "seg", [(s, s + 1) for s in range(count - 1)])
    backward, bsum = call(
        backward_kernel,
        "backward",
        (table,),
        (both, kron, rows),
        (),
        [vmem(*flat), vmem(8, LANES)],
        [pltpu.VMEM(chunk, F32)],
    )
    product, sums = call(
        product_kernel,
        "product",
        (seg,),
        (received, backward, fsum, bsum),
        (first,),
        [vmem(*flat), vmem(groups, 1, LANES)],
        [pltpu.VMEM(flat, F32), pltpu.SemaphoreType.DMA(())],
    )
    whole = (ANY, jax.ShapeDtypeStruct(flat, F32))
    forward, backward, posterior, logs = call(
        scale_kernel,
        "scale",
        (),
        (exchanged(sums), forward, backward, product),
        (),
        [whole, whole, whole, (VMEM, jax.ShapeDtypeStruct((1, 2), F32))],
        [pltpu.VMEM((3, *flat), F32), pltpu.SemaphoreType.DMA((3, 2))],
    )
    return (
        forward.reshape(1, -1),
        backward.reshape(1, -1),
        posterior.reshape(1, -1),
        logs.reshape(2, 1),
    )


def solution(mesh):
    placed = (P("seg", "state"), P("seg", "state"), P("seg", None), P("seg", None))
    return jax.shard_map(
        shards,
        mesh=mesh,
        in_specs=placed,
        out_specs=(P("seg", "state"), P("seg", "state"), P("seg", "state"), P(None, "seg")),
        check_vma=False,
    )
```

time: 130 us -> 122 us (0.938)
  Pallas kernels: 18.6 us -> 12.8 us
  local copies, waits for them, and re-layouts: 2.05 us -> 0 us
    pallas_call x6, Pallas kernels: 18.6 us -> 12.8 us  [call(): pl.pallas_call(kernel, name=name, in_specs=[SMEM] * len(scalars) + [VMEM]...]
    unnamed x5 -> x0, local copies, waits for them, and re-layouts: 2.05 us -> none
where the time goes in v2:
time: 122 us; the launch traced here: 121 us
  blocking collectives  99.4 us (81%)
  Pallas kernels  12.8 us (10%)
  waiting for transfers between devices  6.56 us (5%)
  starting transfers between devices  1.92 us (2%)
    all_to_all x3, blocking collectives, exchanged(): lax.all_to_all(blocks, 'state', split_axis=0, concat_axis=0, tiled=True)  99.4 us
    pallas_call x6, Pallas kernels, call(): pl.pallas_call(kernel, name=name, in_specs=[SMEM] * len(scalars) + [VMEM]...  12.8 us
    ppermute x1, waiting for transfers between devices, shards(): lax.ppermute(forward, 'seg', [(s, s + 1) for s in range(count - 1)])  6.56 us
  transfers between devices with their start and end apart: 1, of which 1 were waited for; matrix products, arithmetic and copies ran while one was open for 0% of the time, Pallas kernels for 2%

profile of v2, /device:TPU:6, one launch (start us, length us, event | category | flops | bytes accessed | tf_op | source)
XLA Modules:
  0.0 121.4 jit_solution(11405160103517727710)
XLA Ops:
  0.6 5.2 %first.1 = (f32[64,32,128]{2,1,0:T(8,128)S(1)}, f32[128]{0:T(128)}, f32[2,16,128]{2,1,0:T(8,128)S(1)}, bf16[2,2,128,128]{3,2,1,0:T(8,128)(2,1)S(1)}, bf16[3,2,128,128]{3,2,1,0:T(8,128)(2,1)S(1)}) custom-call(s32[2,23]{1,0:T(2,128)} %theta_ref.1, s32[2,23]{1,0:T(2,128)} %mask_ref.1, s32[1]{0:T(128)} %bitcast.1.device_ref, f32[1024,128]{1,0:T(8,128)} %bitcast.8, ...), custom_call_target="tpu_custom_call" | custom-call | tf_op jit(solution)/shard_map/first/pallas_call | solution.py:316
  5.8 46.1 %all_to_all.15.in_ref = f32[64,32,128]{2,1,0:T(8,128)S(1)} all-to-all(f32[64,32,128]{2,1,0:T(8,128)S(1)} %get-tuple-element.20), channel_id=1, replica_groups=mesh['seg'=8,'state'=64] {'state'}, dimensions={0} | all-to-all | bytes 2097152 | tf_op jit(solution)/shard_map/all_to_all | solution.py:312
  52.0 2.5 %second.1 = f32[64,32,128]{2,1,0:T(8,128)S(1)} custom-call(f32[128]{0:T(128)} %get-tuple-element.19.table_ref, f32[64,32,128]{2,1,0:T(8,128)S(1)} %all_to_all.15.in_ref, f32[2,16,128]{2,1,0:T(8,128)S(1)} %get-tuple-element.21.low_ref, bf16[2,2,128,128]{3,2,1,0:T(8,128)(2,1)S(1)} %get-tuple-element.22.kron_ref, ...), custom_call_target="tpu_custom_call" | custom-call | tf_op jit(solution)/shard_map/second/pallas_call | solution.py:316
  54.5 35.2 %all_to_all.16.in_ref = f32[64,32,128]{2,1,0:T(8,128)S(1)} all-to-all(f32[64,32,128]{2,1,0:T(8,128)S(1)} %second.1), channel_id=1, replica_groups=mesh['seg'=8,'state'=64] {'state'}, dimensions={0} | all-to-all | bytes 2097152 | tf_op jit(solution)/shard_map/all_to_all | solution.py:312
  89.7 1.0 forward.1
  90.7 1.9 %collective-permute-start = (f32[1024,128]{1,0:T(8,128)S(1)}, f32[1024,128]{1,0:T(8,128)S(1)}, u32[]{:S(2)}, u32[]{:S(2)}) collective-permute-start(f32[1024,128]{1,0:T(8,128)S(1)} %get-tuple-element.24.fwd_ref), channel_id=1, source_target_pairs={{0,64},{64,128},{128,192},{192,256},{256,320},{320,384},{384,448},... | collective-permute-start | bytes 1572872 | tf_op jit(solution)/shard_map/ppermute | solution.py:375
  92.6 2.0 %backward.1 = (f32[1024,128]{1,0:T(8,128)S(1)}, f32[8,128]{1,0:T(8,128)S(1)}) custom-call(f32[128]{0:T(128)} %get-tuple-element.19.table_ref, f32[64,32,128]{2,1,0:T(8,128)S(1)} %all_to_all.16.in_ref, bf16[2,2,128,128]{3,2,1,0:T(8,128)(2,1)S(1)} %get-tuple-element.22.kron_ref, bf16[3,2,128,128]{3,2,1,0:T(8,128)(2,1)S(1)} %get-tuple-element.23.rows_ref), custom_call_target="tpu_custom_call" | custom-call | tf_op jit(solution)/shard_map/backward/pallas_call | solution.py:316
  94.6 6.6 %collective-permute-done.got_ref = f32[1024,128]{1,0:T(8,128)S(1)} collective-permute-done((f32[1024,128]{1,0:T(8,128)S(1)}, f32[1024,128]{1,0:T(8,128)S(1)}, u32[]{:S(2)}, u32[]{:S(2)}) %collective-permute-start) | collective-permute-done | bytes 524320 | tf_op jit(solution)/shard_map/ppermute | solution.py:375
  101.2 0.2 product.1
  101.4 18.1 %all_to_all.17.total_ref = f32[64,1,128]{2,1,0:T(1,128)S(1)} all-to-all(f32[64,1,128]{2,1,0:T(1,128)S(1)} %get-tuple-element.28), channel_id=1, replica_groups=mesh['seg'=8,'state'=64] {'state'}, dimensions={0} | all-to-all | bytes 65536 | tf_op jit(solution)/shard_map/all_to_all | solution.py:312
  119.5 1.9 %scale.1 = (f32[1024,128]{1,0:T(8,128)}, f32[1024,128]{1,0:T(8,128)}, f32[1024,128]{1,0:T(8,128)}, f32[1,2]{1,0:T(1,128)}) custom-call(f32[64,1,128]{2,1,0:T(1,128)S(1)} %all_to_all.17.total_ref, f32[1024,128]{1,0:T(8,128)S(1)} %get-tuple-element.24.fwd_ref, f32[1024,128]{1,0:T(8,128)S(1)} %get-tuple-element.25.bwd_ref, ...), custom_call_target="tpu_custom_call" | custom-call | tf_op jit(solution)/shard_map/scale/pallas_call | solution.py:316
Async XLA Ops:
  90.7 10.5 %collective-permute-start = (f32[1024,128]{1,0:T(8,128)S(1)}, f32[1024,128]{1,0:T(8,128)S(1)}, u32[]{:S(2)}, u32[]{:S(2)}) collective-permute-start(f32[1024,128]{1,0:T(8,128)S(1)} %get-tuple-element.24.fwd_ref), channel_id=1, source_target_pairs={{0,64},{64,128},{128,192},{192,256},{256,320},{320,384},{384,448},... | collective-permute-start | bytes 1572872 | tf_op jit(solution)/shard_map/ppermute | solution.py:375

commit v3 on v2

--- a/solution.py
+++ b/solution.py
@@ -26,8 +26,8 @@
     pairs = []
     for b in range(MEIOSES):
         mask = mask_ref[marker, b]
-        zero = jnp.where(mask % 2 == 1, F32(1.0), F32(PENALTY))
-        one = jnp.where(mask // 2 == 1, F32(1.0), F32(PENALTY))
+        zero = jnp.where(mask & 1 == 1, F32(1.0), F32(PENALTY))
+        one = jnp.where(mask >> 1 == 1, F32(1.0), F32(PENALTY))
         pairs.append((zero, one))
     return pairs
 
@@ -67,11 +67,13 @@
 
 
 def mix_blocks(chunks, lanes, rows):
+    count = len(chunks) // 8
     mixed = mix_lanes(jnp.concatenate(chunks, axis=0), lanes)
-    mixed = mix_row_bits(rows, jnp.concatenate([mixed[:128], mixed[128:]], axis=1))
+    side_by_side = jnp.concatenate([mixed[i * 128 : (i + 1) * 128] for i in range(count)], axis=1)
+    mixed = mix_row_bits(rows, side_by_side)
     return [
-        mixed[j * ROWS : (j + 1) * ROWS, half * LANES : (half + 1) * LANES]
-        for half in range(2)
+        mixed[j * ROWS : (j + 1) * ROWS, i * LANES : (i + 1) * LANES]
+        for i in range(count)
         for j in range(8)
     ]
 
@@ -120,20 +122,28 @@
     return low_factor(anchors) * device_factor(anchors, first_device, device)
 
 
-THETAS, FACTORS, TABLE = 0, 64, 128
+THETAS, FACTORS, TABLE = 0, 64, 96
+PARTS = 1
 
 
 def table_thetas(table_ref, marker):
-    return [table_ref[THETAS + 32 * marker + b] for b in range(MEIOSES)]
+    return [table_ref[pl.ds(THETAS + 32 * marker + b, 1), :] for b in range(MEIOSES)]
 
 
 def emitted(table_ref, low_ref, layout, i, j):
-    scalar = table_ref[FACTORS + 16 * layout + i] * table_ref[FACTORS + 16 * layout + 8 + j]
-    return ERROR_RATE + scalar * low_ref[layout]
-
-
-def first_kernel(theta_ref, mask_ref, device_ref, fwd_ref, bwd_ref, out_ref, table_ref, low_ref, kron_ref, rows_ref,
-                 fwd_in, bwd_in, tmp, sems):
+    outer = table_ref[pl.ds(FACTORS + 16 * layout + i, 1), :]
+    inner = table_ref[pl.ds(FACTORS + 16 * layout + 8 + j, 1), :]
+    return ERROR_RATE + (outer * inner) * low_ref[layout]
+
+
+def first_kernel(theta_hbm, mask_hbm, fwd_ref, bwd_ref, out_ref, table_ref, low_ref, kron_ref, rows_ref,
+                 theta_ref, mask_ref, fwd_in, bwd_in, tmp, small, sems):
+    scalars = [
+        pltpu.make_async_copy(source, target, small.at[k])
+        for k, (source, target) in enumerate(((theta_hbm, theta_ref), (mask_hbm, mask_ref)))
+    ]
+    for copy in scalars:
+        copy.start()
     copies = [
         [
             pltpu.make_async_copy(
@@ -146,17 +156,19 @@
     for row in copies:
         for copy in row:
             copy.start()
-    device = device_ref[0]
+    device = lax.axis_index("state")
+    for copy in scalars:
+        copy.wait()
     thetas = [theta_list(theta_ref, m) for m in range(2)]
     for m in range(2):
         for b in range(MEIOSES):
-            table_ref[THETAS + 32 * m + b] = thetas[m][b]
+            table_ref[pl.ds(THETAS + 32 * m + b, 1), :] = jnp.full((1, LANES), thetas[m][b], F32)
     for layout, (marker, chunk, own) in enumerate(((0, HIGH, MID), (1, MID, HIGH))):
         anchors = anchor_list(mask_ref, marker)
         low_ref[layout] = low_table(anchors, own, device)
         for at, bits in ((0, chunk + 3), (8, chunk)):
             for i, value in enumerate(three_bits(anchors, bits)):
-                table_ref[FACTORS + 16 * layout + at + i] = value
+                table_ref[pl.ds(FACTORS + 16 * layout + at + i, 1), :] = jnp.full((1, LANES), value, F32)
     for m in range(2):
         for part, value in enumerate(two_parts(kron_rows(thetas[m][:7]))):
             kron_ref[m, part] = value
@@ -165,17 +177,19 @@
     for part, value in enumerate(two_parts(kron_rows(thetas[1][7:11] + thetas[1][17:20]))):
         rows_ref[2, part] = value
     for which, source in enumerate((fwd_in, bwd_in)):
-        for p in range(4):
-            copies[which][p].wait()
-            chunks = [source[pl.ds(p * 256 + k * ROWS, ROWS), :] for k in range(16)]
+        for copy in copies[which]:
+            copy.wait()
+        for p in range(PARTS):
+            first = p * 64 // PARTS
+            chunks = [source[pl.ds((first + k) * ROWS, ROWS), :] for k in range(64 // PARTS)]
             if which == 1:
                 chunks = [
-                    chunks[k] * emitted(table_ref, low_ref, 1, 2 * p + k // 8, k % 8)
-                    for k in range(16)
+                    chunk * emitted(table_ref, low_ref, 1, (first + k) // 8, k % 8)
+                    for k, chunk in enumerate(chunks)
                 ]
             chunks = mix_blocks(chunks, kron_ref[which], rows_ref[which])
-            for k in range(16):
-                tmp[which, 16 * p + k] = chunks[k]
+            for k, chunk in enumerate(chunks):
+                tmp[which, first + k] = chunk
         for j in range(8):
             chunks = butterfly([tmp[which, 8 * i + j] for i in range(8)], thetas[which][14:17])
             for i in range(8):
@@ -191,9 +205,10 @@
             chunks = butterfly([in_ref[8 * i + j, rows, :] for i in range(8)], before[20:23])
             for i in range(8):
                 tmp[which, 8 * i + j] = chunks[i]
-        for pair in range(4):
+        for p in range(PARTS):
+            first = p * 64 // PARTS
             both = []
-            for i in (2 * pair, 2 * pair + 1):
+            for i in range(first // 8, (first + 64 // PARTS) // 8):
                 chunks = butterfly([tmp[which, 8 * i + j] for j in range(8)], before[17:20])
                 chunks = [chunks[j] * emitted(table_ref, low_ref, 0, i, j) for j in range(8)]
                 if which == 1:
@@ -201,8 +216,8 @@
                 both += chunks
             if which == 0:
                 both = mix_blocks(both, kron_ref[1], rows_ref[2])
-            for k in range(16):
-                tmp[which, 16 * pair + k] = both[k]
+            for k, chunk in enumerate(both):
+                tmp[which, first + k] = chunk
         for j in range(8):
             chunks = butterfly([tmp[which, 8 * i + j] for i in range(8)], after[20:23])
             for i in range(8):
@@ -227,11 +242,11 @@
 
 def backward_kernel(table_ref, in_ref, kron_ref, rows_ref, out_ref, sum_ref, tmp):
     thetas = table_thetas(table_ref, 0)
-    for p in range(4):
-        chunks = [in_ref[16 * p + k, pl.ds(ROWS, ROWS), :] for k in range(16)]
-        chunks = mix_blocks(chunks, kron_ref[0], rows_ref[0])
-        for k in range(16):
-            tmp[16 * p + k] = chunks[k]
+    for p in range(PARTS):
+        first = p * 64 // PARTS
+        chunks = [in_ref[first + k, pl.ds(ROWS, ROWS), :] for k in range(64 // PARTS)]
+        for k, chunk in enumerate(mix_blocks(chunks, kron_ref[0], rows_ref[0])):
+            tmp[first + k] = chunk
     acc = jnp.zeros((ROWS, LANES), F32)
     for j in range(8):
         chunks = butterfly([tmp[8 * i + j] for i in range(8)], thetas[14:17])
@@ -241,8 +256,8 @@
     sum_ref[...] = acc[:8] + acc[8:]
 
 
-def product_kernel(seg_ref, got_ref, bwd_ref, fsum_ref, bsum_ref, first_ref, out_ref, sum_ref, first_in, sem):
-    is_first = seg_ref[0] == 0
+def product_kernel(got_ref, bwd_ref, fsum_ref, bsum_ref, first_ref, _, out_ref, sum_ref, first_in, sem):
+    is_first = lax.axis_index("seg") == 0
 
     @pl.when(is_first)
     def _():
@@ -295,7 +310,6 @@
         copy.wait()
 
 
-SMEM = pl.BlockSpec(memory_space=pltpu.SMEM)
 VMEM = pl.BlockSpec(memory_space=pltpu.VMEM)
 ANY = pl.BlockSpec(memory_space=pl.ANY)
 
@@ -312,15 +326,15 @@
     return lax.all_to_all(blocks, "state", split_axis=0, concat_axis=0, tiled=True)
 
 
-def call(kernel, name, scalars, vectors, raw, outs, scratch=()):
+def call(kernel, name, vectors, raw, outs, scratch=()):
     return pl.pallas_call(
         kernel,
         name=name,
-        in_specs=[SMEM] * len(scalars) + [VMEM] * len(vectors) + [ANY] * len(raw),
+        in_specs=[VMEM] * len(vectors) + [ANY] * len(raw),
         out_specs=[o[0] for o in outs],
         out_shape=[o[1] for o in outs],
         scratch_shapes=scratch,
-    )(*scalars, *[kept(v) for v in vectors], *raw)
+    )(*[kept(v) for v in vectors], *raw)
 
 
 def shards(forward_in, backward_in, compat_masks, theta_index):
@@ -328,26 +342,26 @@
     pair = (groups, 2 * ROWS, LANES)
     flat = (groups * ROWS, LANES)
     chunk = (groups, ROWS, LANES)
-    device = lax.axis_index("state").reshape(1)
-    seg = lax.axis_index("seg").reshape(1)
     first = forward_in.reshape(flat)
     both, table, low, kron, rows = call(
         first_kernel,
         "first",
-        (theta_index, compat_masks, device),
         (),
-        (first, backward_in.reshape(flat)),
+        (theta_index, compat_masks, first, backward_in.reshape(flat)),
         [
             vmem(*pair),
-            (SMEM, jax.ShapeDtypeStruct((TABLE,), F32)),
+            vmem(TABLE, LANES),
             vmem(2, ROWS, LANES),
             vmem(2, 2, LANES, LANES, dtype=BF16),
             vmem(3, 2, LANES, LANES, dtype=BF16),
         ],
         [
+            pltpu.SMEM(theta_index.shape, jnp.int32),
+            pltpu.SMEM(compat_masks.shape, jnp.int32),
             pltpu.VMEM(flat, F32),
             pltpu.VMEM(flat, F32),
             pltpu.VMEM((2, *chunk), F32),
+            pltpu.SemaphoreType.DMA((2,)),
             pltpu.SemaphoreType.DMA((2, 4)),
         ],
     )
@@ -355,8 +369,7 @@
     (both,) = call(
         second_kernel,
         "second",
-        (table,),
-        (both, low, kron, rows),
+        (table, both, low, kron, rows),
         (),
         [vmem(*pair)],
         [pltpu.VMEM((2, *chunk), F32)],
@@ -365,8 +378,7 @@
     forward, fsum = call(
         forward_kernel,
         "forward",
-        (table,),
-        (both, low),
+        (table, both, low),
         (),
         [vmem(*flat), vmem(8, LANES)],
         [pltpu.VMEM(chunk, F32)],
@@ -376,8 +388,7 @@
     backward, bsum = call(
         backward_kernel,
         "backward",
-        (table,),
-        (both, kron, rows),
+        (table, both, kron, rows),
         (),
         [vmem(*flat), vmem(8, LANES)],
         [pltpu.VMEM(chunk, F32)],
@@ -385,9 +396,8 @@
     product, sums = call(
         product_kernel,
         "product",
-        (seg,),
         (received, backward, fsum, bsum),
-        (first,),
+        (first, lax.axis_index("seg").reshape(1)),
         [vmem(*flat), vmem(groups, 1, LANES)],
         [pltpu.VMEM(flat, F32), pltpu.SemaphoreType.DMA(())],
     )
@@ -395,7 +405,6 @@
     forward, backward, posterior, logs = call(
         scale_kernel,
         "scale",
-        (),
         (exchanged(sums), forward, backward, product),
         (),
         [whole, whole, whole, (VMEM, jax.ShapeDtypeStruct((1, 2), F32))],

time: 122 us -> 118 us (0.967)
  Pallas kernels: 12.8 us -> 7.66 us
    pallas_call x6, Pallas kernels: 12.8 us -> 7.66 us  [call(): pl.pallas_call(kernel, name=name, in_specs=[VMEM] * len(vectors) + [ANY]...]
  transfers between devices with their start and end apart: 1 -> 1, of which waited for: 1 -> 1; matrix products, arithmetic and copies ran while one was open for 0% -> 0% of each run, Pallas kernels for 2% -> 1%
where the time goes in v3:
time: 118 us; the launch traced here: 117 us
  blocking collectives  99.4 us (84%)
  waiting for transfers between devices  7.74 us (7%)
  Pallas kernels  7.66 us (6%)
  starting transfers between devices  1.92 us (2%)
    all_to_all x3, blocking collectives, exchanged(): lax.all_to_all(blocks, 'state', split_axis=0, concat_axis=0, tiled=True)  99.4 us
    ppermute x1, waiting for transfers between devices, shards(): lax.ppermute(forward, 'seg', [(s, s + 1) for s in range(count - 1)])  7.74 us
    pallas_call x6, Pallas kernels, call(): pl.pallas_call(kernel, name=name, in_specs=[VMEM] * len(vectors) + [ANY]...  7.66 us
  transfers between devices with their start and end apart: 1, of which 1 were waited for; matrix products, arithmetic and copies ran while one was open for 0% of the time, Pallas kernels for 1%

profile of v3, /device:TPU:6, one launch (start us, length us, event | category | flops | bytes accessed | tf_op | source)
XLA Modules:
  0.0 117.4 jit_solution(6328314508566359723)
XLA Ops:
  0.6 3.1 %first.1 = (f32[64,32,128]{2,1,0:T(8,128)S(1)}, f32[96,128]{1,0:T(8,128)S(1)}, f32[2,16,128]{2,1,0:T(8,128)S(1)}, bf16[2,2,128,128]{3,2,1,0:T(8,128)(2,1)S(1)}, bf16[3,2,128,128]{3,2,1,0:T(8,128)(2,1)S(1)}) custom-call(s32[2,23]{1,0:T(2,128)} %theta_hbm.1, s32[2,23]{1,0:T(2,128)} %mask_hbm.1, f32[1024,128]{1,0:T(8,128)} %bitcast.7, f32[1024,128]{1,0:T(8,128)} %bitcast.9), custom_call_target="tpu_custom_call" | custom-call | tf_op jit(solution)/shard_map/first/pallas_call | solution.py:330
  3.7 46.1 %all_to_all.15.in_ref = f32[64,32,128]{2,1,0:T(8,128)S(1)} all-to-all(f32[64,32,128]{2,1,0:T(8,128)S(1)} %get-tuple-element.20), channel_id=1, replica_groups=mesh['seg'=8,'state'=64] {'state'}, dimensions={0} | all-to-all | bytes 2097152 | tf_op jit(solution)/shard_map/all_to_all | solution.py:326
  49.8 1.4 %second.1 = f32[64,32,128]{2,1,0:T(8,128)S(1)} custom-call(f32[96,128]{1,0:T(8,128)S(1)} %get-tuple-element.19.table_ref, f32[64,32,128]{2,1,0:T(8,128)S(1)} %all_to_all.15.in_ref, f32[2,16,128]{2,1,0:T(8,128)S(1)} %get-tuple-element.21.low_ref, bf16[2,2,128,128]{3,2,1,0:T(8,128)(2,1)S(1)} %get-tuple-element.22.kron_ref, ...), custom_call_target="tpu_custom_call" | custom-call | tf_op jit(solution)/shard_map/second/pallas_call | solution.py:330
  51.2 35.2 %all_to_all.16.in_ref = f32[64,32,128]{2,1,0:T(8,128)S(1)} all-to-all(f32[64,32,128]{2,1,0:T(8,128)S(1)} %second.1), channel_id=1, replica_groups=mesh['seg'=8,'state'=64] {'state'}, dimensions={0} | all-to-all | bytes 2097152 | tf_op jit(solution)/shard_map/all_to_all | solution.py:326
  86.4 0.3 forward.1
  86.7 1.9 %collective-permute-start = (f32[1024,128]{1,0:T(8,128)S(1)}, f32[1024,128]{1,0:T(8,128)S(1)}, u32[]{:S(2)}, u32[]{:S(2)}) collective-permute-start(f32[1024,128]{1,0:T(8,128)S(1)} %get-tuple-element.24.fwd_ref), channel_id=1, source_target_pairs={{0,64},{64,128},{128,192},{192,256},{256,320},{320,384},{384,448},... | collective-permute-start | bytes 1572872 | tf_op jit(solution)/shard_map/ppermute | solution.py:387
  88.7 0.8 backward.1
  89.5 7.7 %collective-permute-done.got_ref = f32[1024,128]{1,0:T(8,128)S(1)} collective-permute-done((f32[1024,128]{1,0:T(8,128)S(1)}, f32[1024,128]{1,0:T(8,128)S(1)}, u32[]{:S(2)}, u32[]{:S(2)}) %collective-permute-start) | collective-permute-done | bytes 524320 | tf_op jit(solution)/shard_map/ppermute | solution.py:387
  97.2 0.2 product.1
  97.4 18.1 %all_to_all.17.total_ref = f32[64,1,128]{2,1,0:T(1,128)S(1)} all-to-all(f32[64,1,128]{2,1,0:T(1,128)S(1)} %get-tuple-element.28), channel_id=1, replica_groups=mesh['seg'=8,'state'=64] {'state'}, dimensions={0} | all-to-all | bytes 65536 | tf_op jit(solution)/shard_map/all_to_all | solution.py:326
  115.6 1.9 %scale.1 = (f32[1024,128]{1,0:T(8,128)}, f32[1024,128]{1,0:T(8,128)}, f32[1024,128]{1,0:T(8,128)}, f32[1,2]{1,0:T(1,128)}) custom-call(f32[64,1,128]{2,1,0:T(1,128)S(1)} %all_to_all.17.total_ref, f32[1024,128]{1,0:T(8,128)S(1)} %get-tuple-element.24.fwd_ref, f32[1024,128]{1,0:T(8,128)S(1)} %get-tuple-element.25.bwd_ref, ...), custom_call_target="tpu_custom_call" | custom-call | tf_op jit(solution)/shard_map/scale/pallas_call | solution.py:330
Async XLA Ops:
  86.7 10.5 %collective-permute-start = (f32[1024,128]{1,0:T(8,128)S(1)}, f32[1024,128]{1,0:T(8,128)S(1)}, u32[]{:S(2)}, u32[]{:S(2)}) collective-permute-start(f32[1024,128]{1,0:T(8,128)S(1)} %get-tuple-element.24.fwd_ref), channel_id=1, source_target_pairs={{0,64},{64,128},{128,192},{192,256},{256,320},{320,384},{384,448},... | collective-permute-start | bytes 1572872 | tf_op jit(solution)/shard_map/ppermute | solution.py:387

commit v4 on v3

--- a/solution.py
+++ b/solution.py
@@ -53,17 +53,17 @@
 
 
 def mix_lanes(x, kron):
-    high, low = two_parts(x)
-    left = jnp.concatenate([high, low, high, low], axis=1)
-    right = jnp.concatenate([kron[0], kron[0], kron[1], kron[1]], axis=0)
-    return jnp.dot(left, right, preferred_element_type=F32)
+    left = jnp.concatenate(two_parts(x), axis=1)
+    once = jnp.concatenate([kron[0], kron[1]], axis=1)
+    both = jnp.dot(left, jnp.concatenate([once, once], axis=0), preferred_element_type=F32)
+    return both[:, :LANES] + both[:, LANES:]
 
 
 def mix_row_bits(kron, x):
-    high, low = two_parts(x)
-    left = jnp.concatenate([kron[0], kron[0], kron[1], kron[1]], axis=1)
-    right = jnp.concatenate([high, low, high, low], axis=0)
-    return jnp.dot(left, right, preferred_element_type=F32)
+    right = jnp.concatenate(two_parts(x), axis=0)
+    once = jnp.concatenate([kron[0], kron[1]], axis=0)
+    both = jnp.dot(jnp.concatenate([once, once], axis=1), right, preferred_element_type=F32)
+    return both[:128] + both[128:]
 
 
 def mix_blocks(chunks, lanes, rows):
@@ -145,12 +145,7 @@
     for copy in scalars:
         copy.start()
     copies = [
-        [
-            pltpu.make_async_copy(
-                source.at[pl.ds(p * 256, 256), :], target.at[pl.ds(p * 256, 256), :], sems.at[which, p]
-            )
-            for p in range(4)
-        ]
+        [pltpu.make_async_copy(source, target, sems.at[which])]
         for which, (source, target) in enumerate(((fwd_ref, fwd_in), (bwd_ref, bwd_in)))
     ]
     for row in copies:
@@ -176,9 +171,9 @@
             rows_ref[m, part] = value
     for part, value in enumerate(two_parts(kron_rows(thetas[1][7:11] + thetas[1][17:20]))):
         rows_ref[2, part] = value
+    for row in copies:
+        row[0].wait()
     for which, source in enumerate((fwd_in, bwd_in)):
-        for copy in copies[which]:
-            copy.wait()
         for p in range(PARTS):
             first = p * 64 // PARTS
             chunks = [source[pl.ds((first + k) * ROWS, ROWS), :] for k in range(64 // PARTS)]
@@ -362,7 +357,7 @@
             pltpu.VMEM(flat, F32),
             pltpu.VMEM((2, *chunk), F32),
             pltpu.SemaphoreType.DMA((2,)),
-            pltpu.SemaphoreType.DMA((2, 4)),
+            pltpu.SemaphoreType.DMA((2,)),
         ],
     )
     both = exchanged(both)

time: 118 us -> 117 us (level)
  no operation moved by 1% of the time
where the time goes in v4:
time: 117 us; the launch traced here: 116 us
  blocking collectives  99.4 us (85%)
  waiting for transfers between devices  7.88 us (7%)
  Pallas kernels  6.57 us (6%)
  starting transfers between devices  1.92 us (2%)
    all_to_all x3, blocking collectives, exchanged(): lax.all_to_all(blocks, 'state', split_axis=0, concat_axis=0, tiled=True)  99.4 us
    ppermute x1, waiting for transfers between devices, shards(): lax.ppermute(forward, 'seg', [(s, s + 1) for s in range(count - 1)])  7.88 us
    pallas_call x6, Pallas kernels, call(): pl.pallas_call(kernel, name=name, in_specs=[VMEM] * len(vectors) + [ANY]...  6.57 us
  transfers between devices with their start and end apart: 1, of which 1 were waited for; matrix products, arithmetic and copies ran while one was open for 0% of the time, Pallas kernels for 1%

profile of v4, /device:TPU:6, one launch (start us, length us, event | category | flops | bytes accessed | tf_op | source)
XLA Modules:
  0.0 116.5 jit_solution(17822394035131044111)
XLA Ops:
  0.6 2.2 %first.1 = (f32[64,32,128]{2,1,0:T(8,128)S(1)}, f32[96,128]{1,0:T(8,128)S(1)}, f32[2,16,128]{2,1,0:T(8,128)S(1)}, bf16[2,2,128,128]{3,2,1,0:T(8,128)(2,1)S(1)}, bf16[3,2,128,128]{3,2,1,0:T(8,128)(2,1)S(1)}) custom-call(s32[2,23]{1,0:T(2,128)} %theta_hbm.1, s32[2,23]{1,0:T(2,128)} %mask_hbm.1, f32[1024,128]{1,0:T(8,128)} %bitcast.7, f32[1024,128]{1,0:T(8,128)} %bitcast.9), custom_call_target="tpu_custom_call" | custom-call | tf_op jit(solution)/shard_map/first/pallas_call | solution.py:325
  2.9 46.1 %all_to_all.15.in_ref = f32[64,32,128]{2,1,0:T(8,128)S(1)} all-to-all(f32[64,32,128]{2,1,0:T(8,128)S(1)} %get-tuple-element.20), channel_id=1, replica_groups=mesh['seg'=8,'state'=64] {'state'}, dimensions={0} | all-to-all | bytes 2097152 | tf_op jit(solution)/shard_map/all_to_all | solution.py:321
  49.0 1.3 %second.1 = f32[64,32,128]{2,1,0:T(8,128)S(1)} custom-call(f32[96,128]{1,0:T(8,128)S(1)} %get-tuple-element.19.table_ref, f32[64,32,128]{2,1,0:T(8,128)S(1)} %all_to_all.15.in_ref, f32[2,16,128]{2,1,0:T(8,128)S(1)} %get-tuple-element.21.low_ref, bf16[2,2,128,128]{3,2,1,0:T(8,128)(2,1)S(1)} %get-tuple-element.22.kron_ref, ...), custom_call_target="tpu_custom_call" | custom-call | tf_op jit(solution)/shard_map/second/pallas_call | solution.py:325
  50.3 35.2 %all_to_all.16.in_ref = f32[64,32,128]{2,1,0:T(8,128)S(1)} all-to-all(f32[64,32,128]{2,1,0:T(8,128)S(1)} %second.1), channel_id=1, replica_groups=mesh['seg'=8,'state'=64] {'state'}, dimensions={0} | all-to-all | bytes 2097152 | tf_op jit(solution)/shard_map/all_to_all | solution.py:321
  85.4 0.3 forward.1
  85.8 1.9 %collective-permute-start = (f32[1024,128]{1,0:T(8,128)S(1)}, f32[1024,128]{1,0:T(8,128)S(1)}, u32[]{:S(2)}, u32[]{:S(2)}) collective-permute-start(f32[1024,128]{1,0:T(8,128)S(1)} %get-tuple-element.24.fwd_ref), channel_id=1, source_target_pairs={{0,64},{64,128},{128,192},{192,256},{256,320},{320,384},{384,448},... | collective-permute-start | bytes 1572872 | tf_op jit(solution)/shard_map/ppermute | solution.py:382
  87.7 0.7 backward.1
  88.4 7.9 %collective-permute-done.got_ref = f32[1024,128]{1,0:T(8,128)S(1)} collective-permute-done((f32[1024,128]{1,0:T(8,128)S(1)}, f32[1024,128]{1,0:T(8,128)S(1)}, u32[]{:S(2)}, u32[]{:S(2)}) %collective-permute-start) | collective-permute-done | bytes 524320 | tf_op jit(solution)/shard_map/ppermute | solution.py:382
  96.3 0.2 product.1
  96.5 18.1 %all_to_all.17.total_ref = f32[64,1,128]{2,1,0:T(1,128)S(1)} all-to-all(f32[64,1,128]{2,1,0:T(1,128)S(1)} %get-tuple-element.28), channel_id=1, replica_groups=mesh['seg'=8,'state'=64] {'state'}, dimensions={0} | all-to-all | bytes 65536 | tf_op jit(solution)/shard_map/all_to_all | solution.py:321
  114.6 1.9 %scale.1 = (f32[1024,128]{1,0:T(8,128)}, f32[1024,128]{1,0:T(8,128)}, f32[1024,128]{1,0:T(8,128)}, f32[1,2]{1,0:T(1,128)}) custom-call(f32[64,1,128]{2,1,0:T(1,128)S(1)} %all_to_all.17.total_ref, f32[1024,128]{1,0:T(8,128)S(1)} %get-tuple-element.24.fwd_ref, f32[1024,128]{1,0:T(8,128)S(1)} %get-tuple-element.25.bwd_ref, ...), custom_call_target="tpu_custom_call" | custom-call | tf_op jit(solution)/shard_map/scale/pallas_call | solution.py:325
Async XLA Ops:
  85.8 10.5 %collective-permute-start = (f32[1024,128]{1,0:T(8,128)S(1)}, f32[1024,128]{1,0:T(8,128)S(1)}, u32[]{:S(2)}, u32[]{:S(2)}) collective-permute-start(f32[1024,128]{1,0:T(8,128)S(1)} %get-tuple-element.24.fwd_ref), channel_id=1, source_target_pairs={{0,64},{64,128},{128,192},{192,256},{256,320},{320,384},{384,448},... | collective-permute-start | bytes 1572872 | tf_op jit(solution)/shard_map/ppermute | solution.py:382

commit v5 on v4

--- a/solution.py
+++ b/solution.py
@@ -379,7 +379,7 @@
         [pltpu.VMEM(chunk, F32)],
     )
     count = lax.axis_size("seg")
-    received = lax.ppermute(forward, "seg", [(s, s + 1) for s in range(count - 1)])
+    received = lax.ppermute(forward, "seg", [(s, (s + 1) % count) for s in range(count)])
     backward, bsum = call(
         backward_kernel,
         "backward",

time: 117 us -> 116 us (level)
  starting transfers between devices: 1.92 us -> 0.02 us
    ppermute x1, starting transfers between devices: 1.92 us -> 0.02 us  [shards(): lax.ppermute(forward, 'seg', [(s, (s + 1) % count) for s in range(count)])]
where the time goes in v5:
time: 116 us; the launch traced here: 115 us
  blocking collectives  99.4 us (86%)
  waiting for transfers between devices  7.9 us (7%)
  Pallas kernels  6.57 us (6%)
    all_to_all x3, blocking collectives, exchanged(): lax.all_to_all(blocks, 'state', split_axis=0, concat_axis=0, tiled=True)  99.4 us
    ppermute x1, waiting for transfers between devices, shards(): lax.ppermute(forward, 'seg', [(s, (s + 1) % count) for s in range(count)])  7.9 us
    pallas_call x6, Pallas kernels, call(): pl.pallas_call(kernel, name=name, in_specs=[VMEM] * len(vectors) + [ANY]...  6.57 us
  transfers between devices with their start and end apart: 1, of which 1 were waited for; matrix products, arithmetic and copies ran while one was open for 0% of the time, Pallas kernels for 1%

profile of v5, /device:TPU:6, one launch (start us, length us, event | category | flops | bytes accessed | tf_op | source)
XLA Modules:
  0.0 114.6 jit_solution(8500662358183843923)
XLA Ops:
  0.6 2.2 %first.1 = (f32[64,32,128]{2,1,0:T(8,128)S(1)}, f32[96,128]{1,0:T(8,128)S(1)}, f32[2,16,128]{2,1,0:T(8,128)S(1)}, bf16[2,2,128,128]{3,2,1,0:T(8,128)(2,1)S(1)}, bf16[3,2,128,128]{3,2,1,0:T(8,128)(2,1)S(1)}) custom-call(s32[2,23]{1,0:T(2,128)} %theta_hbm.1, s32[2,23]{1,0:T(2,128)} %mask_hbm.1, f32[1024,128]{1,0:T(8,128)} %bitcast.7, f32[1024,128]{1,0:T(8,128)} %bitcast.9), custom_call_target="tpu_custom_call" | custom-call | tf_op jit(solution)/shard_map/first/pallas_call | solution.py:325
  2.9 46.1 %all_to_all.15.in_ref = f32[64,32,128]{2,1,0:T(8,128)S(1)} all-to-all(f32[64,32,128]{2,1,0:T(8,128)S(1)} %get-tuple-element.20), channel_id=1, replica_groups=mesh['seg'=8,'state'=64] {'state'}, dimensions={0} | all-to-all | bytes 2097152 | tf_op jit(solution)/shard_map/all_to_all | solution.py:321
  49.0 1.3 %second.1 = f32[64,32,128]{2,1,0:T(8,128)S(1)} custom-call(f32[96,128]{1,0:T(8,128)S(1)} %get-tuple-element.19.table_ref, f32[64,32,128]{2,1,0:T(8,128)S(1)} %all_to_all.15.in_ref, f32[2,16,128]{2,1,0:T(8,128)S(1)} %get-tuple-element.21.low_ref, bf16[2,2,128,128]{3,2,1,0:T(8,128)(2,1)S(1)} %get-tuple-element.22.kron_ref, ...), custom_call_target="tpu_custom_call" | custom-call | tf_op jit(solution)/shard_map/second/pallas_call | solution.py:325
  50.3 35.2 %all_to_all.16.in_ref = f32[64,32,128]{2,1,0:T(8,128)S(1)} all-to-all(f32[64,32,128]{2,1,0:T(8,128)S(1)} %second.1), channel_id=1, replica_groups=mesh['seg'=8,'state'=64] {'state'}, dimensions={0} | all-to-all | bytes 2097152 | tf_op jit(solution)/shard_map/all_to_all | solution.py:321
  85.4 0.3 forward.1
  85.8 0.0 collective-permute-start
  85.8 0.7 backward.1
  86.5 7.9 %collective-permute-done.got_ref = f32[1024,128]{1,0:T(8,128)S(1)} collective-permute-done((f32[1024,128]{1,0:T(8,128)S(1)}, f32[1024,128]{1,0:T(8,128)S(1)}, u32[]{:S(2)}, u32[]{:S(2)}) %collective-permute-start) | collective-permute-done | bytes 524320 | tf_op jit(solution)/shard_map/ppermute | solution.py:382
  94.4 0.2 product.1
  94.6 18.1 %all_to_all.17.total_ref = f32[64,1,128]{2,1,0:T(1,128)S(1)} all-to-all(f32[64,1,128]{2,1,0:T(1,128)S(1)} %get-tuple-element.28), channel_id=1, replica_groups=mesh['seg'=8,'state'=64] {'state'}, dimensions={0} | all-to-all | bytes 65536 | tf_op jit(solution)/shard_map/all_to_all | solution.py:321
  112.7 1.9 %scale.1 = (f32[1024,128]{1,0:T(8,128)}, f32[1024,128]{1,0:T(8,128)}, f32[1024,128]{1,0:T(8,128)}, f32[1,2]{1,0:T(1,128)}) custom-call(f32[64,1,128]{2,1,0:T(1,128)S(1)} %all_to_all.17.total_ref, f32[1024,128]{1,0:T(8,128)S(1)} %get-tuple-element.24.fwd_ref, f32[1024,128]{1,0:T(8,128)S(1)} %get-tuple-element.25.bwd_ref, ...), custom_call_target="tpu_custom_call" | custom-call | tf_op jit(solution)/shard_map/scale/pallas_call | solution.py:325
Async XLA Ops:
  85.8 8.6 %collective-permute-start = (f32[1024,128]{1,0:T(8,128)S(1)}, f32[1024,128]{1,0:T(8,128)S(1)}, u32[]{:S(2)}, u32[]{:S(2)}) collective-permute-start(f32[1024,128]{1,0:T(8,128)S(1)} %get-tuple-element.24.fwd_ref), channel_id=1, source_target_pairs={{0,64},{64,128},{128,192},{192,256},{256,320},{320,384},{384,448},... | collective-permute-start | bytes 1572872 | tf_op jit(solution)/shard_map/ppermute | solution.py:382

commit v6 on v5

--- a/solution.py
+++ b/solution.py
@@ -235,7 +235,9 @@
     sum_ref[...] = acc[:8] + acc[8:]
 
 
-def backward_kernel(table_ref, in_ref, kron_ref, rows_ref, out_ref, sum_ref, tmp):
+def backward_kernel(table_ref, in_ref, kron_ref, rows_ref, first_ref, out_ref, sum_ref, left_ref, tmp, sem):
+    copy = pltpu.make_async_copy(first_ref, left_ref, sem)
+    copy.start()
     thetas = table_thetas(table_ref, 0)
     for p in range(PARTS):
         first = p * 64 // PARTS
@@ -249,16 +251,11 @@
             acc = acc + chunks[i]
             out_ref[pl.ds((8 * i + j) * ROWS, ROWS), :] = chunks[i]
     sum_ref[...] = acc[:8] + acc[8:]
-
-
-def product_kernel(got_ref, bwd_ref, fsum_ref, bsum_ref, first_ref, _, out_ref, sum_ref, first_in, sem):
+    copy.wait()
+
+
+def product_kernel(got_ref, bwd_ref, fsum_ref, bsum_ref, first_ref, out_ref, sum_ref):
     is_first = lax.axis_index("seg") == 0
-
-    @pl.when(is_first)
-    def _():
-        copy = pltpu.make_async_copy(first_ref, first_in, sem)
-        copy.start()
-        copy.wait()
 
     def multiply(left_ref):
         acc = jnp.zeros((8, LANES), F32)
@@ -275,7 +272,7 @@
         )
         sum_ref[...] = jnp.broadcast_to(row[None], sum_ref.shape)
 
-    pl.when(is_first)(lambda: multiply(first_in))
+    pl.when(is_first)(lambda: multiply(first_ref))
     pl.when(jnp.logical_not(is_first))(lambda: multiply(got_ref))
 
 
@@ -322,6 +319,7 @@
 
 
 def call(kernel, name, vectors, raw, outs, scratch=()):
+    raw_in_hbm = len(raw) > 1
     return pl.pallas_call(
         kernel,
         name=name,
@@ -329,6 +327,7 @@
         out_specs=[o[0] for o in outs],
         out_shape=[o[1] for o in outs],
         scratch_shapes=scratch,
+        compiler_params=pltpu.CompilerParams(vmem_limit_bytes=None if raw_in_hbm else 8 << 20),
     )(*[kept(v) for v in vectors], *raw)
 
 
@@ -380,21 +379,20 @@
     )
     count = lax.axis_size("seg")
     received = lax.ppermute(forward, "seg", [(s, (s + 1) % count) for s in range(count)])
-    backward, bsum = call(
+    backward, bsum, left = call(
         backward_kernel,
         "backward",
         (table, both, kron, rows),
-        (),
-        [vmem(*flat), vmem(8, LANES)],
-        [pltpu.VMEM(chunk, F32)],
+        (first,),
+        [vmem(*flat), vmem(8, LANES), vmem(*flat)],
+        [pltpu.VMEM(chunk, F32), pltpu.SemaphoreType.DMA(())],
     )
     product, sums = call(
         product_kernel,
         "product",
-        (received, backward, fsum, bsum),
-        (first, lax.axis_index("seg").reshape(1)),
+        (received, backward, fsum, bsum, left),
+        (),
         [vmem(*flat), vmem(groups, 1, LANES)],
-        [pltpu.VMEM(flat, F32), pltpu.SemaphoreType.DMA(())],
     )
     whole = (ANY, jax.ShapeDtypeStruct(flat, F32))
     forward, backward, posterior, logs = call(

time: 116 us -> 115 us (level)
  no operation moved by 1% of the time
where the time goes in v6:
time: 115 us
  blocking collectives  99.4 us (86%)
  waiting for transfers between devices  7.16 us (6%)
  Pallas kernels  6.61 us (6%)
    all_to_all x3, blocking collectives, exchanged(): lax.all_to_all(blocks, 'state', split_axis=0, concat_axis=0, tiled=True)  99.4 us
    ppermute x1, waiting for transfers between devices, shards(): lax.ppermute(forward, 'seg', [(s, (s + 1) % count) for s in range(count)])  7.16 us
    pallas_call x6, Pallas kernels, call(): pl.pallas_call(kernel, name=name, in_specs=[VMEM] * len(vectors) + [ANY]...  6.61 us
  transfers between devices with their start and end apart: 1, of which 1 were waited for; matrix products, arithmetic and copies ran while one was open for 0% of the time, Pallas kernels for 1%

profile of v6, /device:TPU:6, one launch (start us, length us, event | category | flops | bytes accessed | tf_op | source)
XLA Modules:
  0.0 114.6 jit_solution(7954288533766897625)
XLA Ops:
  0.6 2.2 %first.1 = (f32[64,32,128]{2,1,0:T(8,128)S(1)}, f32[96,128]{1,0:T(8,128)S(1)}, f32[2,16,128]{2,1,0:T(8,128)S(1)}, bf16[2,2,128,128]{3,2,1,0:T(8,128)(2,1)S(1)}, bf16[3,2,128,128]{3,2,1,0:T(8,128)(2,1)S(1)}) custom-call(s32[2,23]{1,0:T(2,128)} %theta_hbm.1, s32[2,23]{1,0:T(2,128)} %mask_hbm.1, f32[1024,128]{1,0:T(8,128)} %bitcast.6, f32[1024,128]{1,0:T(8,128)} %bitcast.8), custom_call_target="tpu_custom_call" | custom-call | tf_op jit(solution)/shard_map/first/pallas_call | solution.py:323
  2.9 46.1 %all_to_all.15.in_ref = f32[64,32,128]{2,1,0:T(8,128)S(1)} all-to-all(f32[64,32,128]{2,1,0:T(8,128)S(1)} %get-tuple-element.21), channel_id=1, replica_groups=mesh['seg'=8,'state'=64] {'state'}, dimensions={0} | all-to-all | bytes 2097152 | tf_op jit(solution)/shard_map/all_to_all | solution.py:318
  49.0 1.3 %second.1 = f32[64,32,128]{2,1,0:T(8,128)S(1)} custom-call(f32[96,128]{1,0:T(8,128)S(1)} %get-tuple-element.20.table_ref, f32[64,32,128]{2,1,0:T(8,128)S(1)} %all_to_all.15.in_ref, f32[2,16,128]{2,1,0:T(8,128)S(1)} %get-tuple-element.22.low_ref, bf16[2,2,128,128]{3,2,1,0:T(8,128)(2,1)S(1)} %get-tuple-element.23.kron_ref, ...), custom_call_target="tpu_custom_call" | custom-call | tf_op jit(solution)/shard_map/second/pallas_call | solution.py:323
  50.3 35.2 %all_to_all.16.in_ref = f32[64,32,128]{2,1,0:T(8,128)S(1)} all-to-all(f32[64,32,128]{2,1,0:T(8,128)S(1)} %second.1), channel_id=1, replica_groups=mesh['seg'=8,'state'=64] {'state'}, dimensions={0} | all-to-all | bytes 2097152 | tf_op jit(solution)/shard_map/all_to_all | solution.py:318
  85.4 0.0 copy-start
  85.4 0.3 forward.1
  85.8 0.0 collective-permute-start
  85.8 0.7 copy-done
  86.5 0.7 backward.1
  87.2 7.2 %collective-permute-done.got_ref = f32[1024,128]{1,0:T(8,128)S(1)} collective-permute-done((f32[1024,128]{1,0:T(8,128)S(1)}, f32[1024,128]{1,0:T(8,128)S(1)}, u32[]{:S(2)}, u32[]{:S(2)}) %collective-permute-start) | collective-permute-done | bytes 524320 | tf_op jit(solution)/shard_map/ppermute | solution.py:381
  94.4 0.2 product.1
  94.6 18.1 %all_to_all.17.total_ref = f32[64,1,128]{2,1,0:T(1,128)S(1)} all-to-all(f32[64,1,128]{2,1,0:T(1,128)S(1)} %get-tuple-element.30), channel_id=1, replica_groups=mesh['seg'=8,'state'=64] {'state'}, dimensions={0} | all-to-all | bytes 65536 | tf_op jit(solution)/shard_map/all_to_all | solution.py:318
  112.7 1.9 %scale.1 = (f32[1024,128]{1,0:T(8,128)}, f32[1024,128]{1,0:T(8,128)}, f32[1024,128]{1,0:T(8,128)}, f32[1,2]{1,0:T(1,128)}) custom-call(f32[64,1,128]{2,1,0:T(1,128)S(1)} %all_to_all.17.total_ref, f32[1024,128]{1,0:T(8,128)S(1)} %get-tuple-element.25.fwd_ref, f32[1024,128]{1,0:T(8,128)S(1)} %get-tuple-element.26.bwd_ref, ...), custom_call_target="tpu_custom_call" | custom-call | tf_op jit(solution)/shard_map/scale/pallas_call | solution.py:323
Async XLA Ops:
  85.4 1.0 copy-start
  85.8 8.6 %collective-permute-start = (f32[1024,128]{1,0:T(8,128)S(1)}, f32[1024,128]{1,0:T(8,128)S(1)}, u32[]{:S(2)}, u32[]{:S(2)}) collective-permute-start(f32[1024,128]{1,0:T(8,128)S(1)} %get-tuple-element.25.fwd_ref), channel_id=1, source_target_pairs={{0,64},{64,128},{128,192},{192,256},{256,320},{320,384},{384,448},... | collective-permute-start | bytes 1572872 | tf_op jit(solution)/shard_map/ppermute | solution.py:381
